TPU v7x, 256 devices: a whole 4x4x8 slice. The times are simulated.
256 devices in a mesh: row: 64 (over x, z_hi, y, core), col: 4 (over z_lo).
Axes of the slice: x: 4, y: 4, z: 8 (z_hi: 2, z_lo: 4; z = z_hi * 4 + z_lo), core: 2. Of those that a mesh axis runs over, the one named last changes fastest.
Arguments:
- matrix: float32 [32, 512, 8, 2048], P(None, 'row', None, 'col'), as said below
Outputs:
- factored: float32 [32, 512, 8, 2048], P(None, 'row', None, 'col')
Inputs may be any that keep to these rules, and one draw needn't show every extreme that they name: `matrix`: symmetric and positive definite.
All inputs are finite; a program needn't handle non-finite values.
Results may differ from a plain program's by a relative error of at most 0.0003.
Values sent between devices are 32-bit elements; how exact they have to be, the bound alone decides.
No kernel may reach another device: no remote copies, remote signals or barrier semaphores. Data moves between devices by JAX's collectives and lax.ppermute only.
A program may use at most 128 MiB of HBM per device.

v0:
```python
import functools

import jax
import jax.numpy as jnp
from jax import lax
from jax.experimental import pallas as pl
from jax.experimental.pallas import tpu as pltpu
from jax.sharding import PartitionSpec as P


W = 512
NB = 128
F32 = jnp.float32
HI = lax.Precision.HIGHEST
ANY = pl.BlockSpec(memory_space=pl.ANY)
VM = pl.BlockSpec(memory_space=pltpu.VMEM)


def swap(value, mask, mask_odd=None):
    mask_odd = mask if mask_odd is None else mask_odd
    pairs = [(r, r ^ (mask_odd if r & 1 else mask)) for r in range(64)]
    return lax.ppermute(value, "row", pairs)


def dot(a, b, da=1, db=0):
    return lax.dot_general(
        a, b, (((da,), (db,)), ((), ())), precision=HI, preferred_element_type=F32
    )


def total(terms):
    while len(terms) > 1:
        pairs = [terms[i] + terms[i + 1] for i in range(0, len(terms) - 1, 2)]
        terms = pairs + terms[2 * len(pairs) :]
    return terms[0]


def factor_block(load, store):
    lane = lax.broadcasted_iota(jnp.int32, (8, NB), 1)
    sub = lax.broadcasted_iota(jnp.int32, (8, NB), 0)
    left = [load(i) for i in range(16)]
    right = [jnp.where(lane == sub + 8 * i, F32(1), F32(0)) for i in range(16)]

    def lanes(v, j):
        return jnp.broadcast_to(v[:, j : j + 1], (8, NB))

    def subs(v, s):
        return jnp.broadcast_to(v[s : s + 1, :], (8, NB))

    for b in range(16):
        more = b < 15
        c = [lanes(left[b], 8 * b + j) for j in range(8)]
        t = {(s, j): subs(c[j], s) for j in range(8) for s in range(j, 8)}
        va = [subs(left[b], s) for s in range(8)] if more else None
        vi = [subs(right[b], s) for s in range(8)]
        nx = [lanes(left[b + 1], 8 * b + j) for j in range(8)] if more else None
        r, d, m = [None] * 8, [None] * 8, {}
        for j in range(8):
            d[j] = t[j, j]
            r[j] = 1.0 / d[j]
            for s in range(j + 1, 8):
                m[s, j] = t[s, j] * r[j]
            for k in range(j + 1, 8):
                for s in range(k, 8):
                    t[s, k] = t[s, k] - m[s, j] * t[k, j]
            for s in range(j + 1, 8):
                if more:
                    va[s] = va[s] - m[s, j] * va[j]
                    nx[s] = nx[s] - m[s, j] * nx[j]
                vi[s] = vi[s] - m[s, j] * vi[j]
        if more:
            wa = [r[s] * va[s] for s in range(8)]
            wi = [r[s] * vi[s] for s in range(8)]
            next_left = left[b + 1] - total([nx[j] * wa[j] for j in range(8)])
            next_right = right[b + 1] - total([nx[j] * wi[j] for j in range(8)])
            for s in range(7, 0, -1):
                for j in range(s):
                    wa[j] = wa[j] - m[s, j] * wa[s]
                    wi[j] = wi[j] - m[s, j] * wi[s]
            for i in range(b + 2, 16):
                ci = [lanes(left[i], 8 * b + j) for j in range(8)]
                left[i] = left[i] - total([ci[j] * wa[j] for j in range(8)])
                right[i] = right[i] - total([ci[j] * wi[j] for j in range(8)])
            left[b + 1], right[b + 1] = next_left, next_right
        out = lax.rsqrt(d[0]) * vi[0]
        for s in range(1, 8):
            out = jnp.where(sub == s, lax.rsqrt(d[s]) * vi[s], out)
        store(b, out)


def identity(work):
    row = lax.broadcasted_iota(jnp.int32, (W, W), 0)
    col = lax.broadcasted_iota(jnp.int32, (W, W), 1)
    work[:, W:] = jnp.where(row == col, F32(1), F32(0))


def factor_steps(work, inv, first, last):
    def step(kb, carry):
        top = pl.multiple_of(kb * NB, NB)
        nxt = pl.multiple_of((kb + 1) * NB, NB)

        def load(i):
            return work[pl.ds(top + 8 * i, 8), pl.ds(top, NB)]

        def store(i, v):
            inv[8 * i : 8 * i + 8, :] = v

        factor_block(load, store)
        work[pl.ds(top, NB), pl.ds(nxt, W)] = dot(
            inv[...], work[pl.ds(top, NB), pl.ds(nxt, W)]
        )

        def update(i, carry):
            at = pl.multiple_of(i * NB, NB)
            work[pl.ds(at, NB), pl.ds(nxt, W)] -= dot(
                work[pl.ds(top, NB), pl.ds(at, NB)],
                work[pl.ds(top, NB), pl.ds(nxt, W)],
                0,
                0,
            )
            return carry

        lax.fori_loop(kb + 1, W // NB, update, 0)
        return carry

    lax.fori_loop(first, last, step, 0)


def lay_out(work, cols, own, other, part):
    core = lax.axis_index("row") % 2
    for x in range(4):
        for y in range(4):
            for z in range(2):
                for source, k in ((own, core), (other, 1 - core)):
                    at = pl.multiple_of(8 * (16 * x + 8 * z + 2 * y + k), 8)
                    work[pl.ds(at, 8), cols] = source[4 * x + y, z, part]


def first_kernel(own, other, x0, work, inv):
    lay_out(work, slice(0, W), own, other, 0)
    identity(work)
    factor_steps(work, inv, 0, 4)
    x0[...] = work[:, W:]


def second_kernel(x0, own, other, u01, x1, work, inv):
    lay_out(work, slice(W, 2 * W), own, other, 0)
    lay_out(work, slice(0, W), own, other, 1)
    u01[...] = dot(x0[...], work[:, W:], 1, 1)
    work[:, :W] -= dot(u01[...], u01[...], 0, 0)
    identity(work)
    factor_steps(work, inv, 0, 4)
    x1[...] = work[:, W:]


def own_rows_kernel(x0, x1, u01, own, s1, s2, s3, b, g, a0, a1, sem):
    c = lax.axis_index("col")
    for dst, sources, k in ((a0, (own, s1, s2, s3), 0), (a1, (s1, own, s3, s2), 1)):
        for i, source in enumerate(sources):

            @pl.when(c == i)
            def _():
                pltpu.make_async_copy(source, dst, sem.at[k]).start()

        pltpu.make_async_copy(own, dst, sem.at[k]).wait()
    b0 = dot(a0[...], x0[...], 1, 1)
    b1 = dot(a1[...] - dot(b0, u01[...]), x1[...], 1, 1)
    g1 = dot(b1, x1[...])
    b[:, :W] = b0
    b[:, W:] = b1
    g[:, W:] = g1
    g[:, :W] = dot(b0 - dot(g1, u01[...], 1, 1), x0[...])


def thirds(v):
    high = v.astype(jnp.bfloat16)
    rest = v - high.astype(F32)
    mid = rest.astype(jnp.bfloat16)
    return high, mid, (rest - mid.astype(F32)).astype(jnp.bfloat16)


def bdot(a, b):
    return lax.dot_general(a, b, (((1,), (0,)), ((), ())), preferred_element_type=F32)


def last_kernel(slots, a, b, g, *rest):
    n = len(slots)
    bufs, out, (held, tile, parts, held_sem, in_sem, out_sem) = rest[:n], rest[n], rest[n + 1 :]
    r, c = lax.axis_index("row"), lax.axis_index("col")
    place = [
        [jnp.bitwise_xor(r, jnp.where((r + k) % 2 == 1, odd, even)) for even, odd, k in ids]
        for ids in slots
    ]

    def fetch(t, carry):
        columns = pl.ds(pl.multiple_of(1024 * t, 1024), 1024)
        for buf, rows in zip(bufs, place):
            for at, block in enumerate(rows):
                for l in range(2):
                    row = pl.multiple_of(8 * (64 * l + block), 8)
                    pltpu.make_async_copy(
                        buf.at[at, l, :, columns], held.at[t, pl.ds(row, 8)], held_sem.at[t]
                    ).start()
        pltpu.make_async_copy(a.at[:, t], tile.at[t], in_sem.at[t]).start()
        return carry

    lax.fori_loop(0, 4, fetch, 0)
    for k, v in enumerate(thirds(g[...])):
        parts[k] = v
    row = lax.broadcasted_iota(jnp.int32, (256, 128), 0)
    col = lax.broadcasted_iota(jnp.int32, (256, 128), 1)
    row_global = (row // 8) * W + r * 8 + row % 8

    def column(t, carry):
        pltpu.make_async_copy(held.at[t], held.at[t], held_sem.at[t]).wait()
        pltpu.make_async_copy(tile.at[t], tile.at[t], in_sem.at[t]).wait()
        flat = tile.at[t].reshape(2048, 128)

        def some(i, carry):
            high, mid, low = thirds(held[t, :, pl.ds(pl.multiple_of(512 * i, 512), 512)])
            product = (
                bdot(parts[0], low)
                + bdot(parts[2], high)
                + bdot(parts[1], mid)
                + bdot(parts[0], mid)
                + bdot(parts[1], high)
                + bdot(parts[0], high)
            )
            for k in range(4):
                m = 4 * i + k
                at = pl.ds(m, 256, stride=8)
                value = flat[at, :] - product[:, 128 * k : 128 * k + 128]
                trailing = (m > 0) | (c >= 2)
                flat[at, :] = jnp.where((row < 16) & trailing, F32(0), value)
            return carry

        lax.fori_loop(0, 2, some, 0)

        @pl.when(c < 2)
        def _():
            at = pl.ds(pl.multiple_of(128 * t, 128), 128)
            ahead = pl.ds(pl.multiple_of(W + 128 * t, 128), 128)
            first, second = b[:, at], b[:, ahead]
            mine = jnp.where(c == 0, first, second)
            flat[pl.ds(0, 256, stride=8), :] = jnp.where(
                row_global - c * W >= col + 128 * t, mine, F32(0)
            )

        pltpu.make_async_copy(tile.at[t], out.at[:, t], out_sem.at[t]).start()
        return carry

    lax.fori_loop(0, 4, column, 0)
    for t in range(4):
        pltpu.make_async_copy(tile.at[t], out.at[:, t], out_sem.at[t]).wait()


def steps(matrix):
    r = lax.axis_index("row")
    c = lax.axis_index("col")
    z_hi = (r // 8) % 2
    tiles = matrix.reshape(256, 8, 4, 128).transpose(0, 2, 1, 3)
    own = matrix[:, :, 0, :].reshape(256, W)

    def by_col(value):
        def send(*pairs):
            return lax.ppermute(value, "col", list(pairs))

        return send((0, 1), (1, 0)), send((0, 2), (1, 3)), send((0, 3), (1, 2))

    groups = [
        [q for q in range(64) if (q // 8) % 2 == z and q % 2 == k] for z in (0, 1) for k in (0, 1)
    ]

    def to_all(value):
        copies = jnp.broadcast_to(value, (16, *value.shape))
        return lax.all_to_all(
            copies, "row", split_axis=0, concat_axis=0, axis_index_groups=groups, tiled=True
        )

    head = own[:16]
    s1, s2, s3 = by_col(head)
    d0 = jnp.where(c == 0, head, jnp.where(c == 1, s1, jnp.where(c == 2, s2, s3)))
    d1 = jnp.where(c == 1, head, jnp.where(c == 0, s1, jnp.where(c == 3, s2, s3)))
    mine = jnp.stack([d0[:8], d0[8:], d1[8:]])
    other = swap(mine, 8)
    both = jnp.where(z_hi == 0, jnp.stack([mine, other]), jnp.stack([other, mine]))
    d00 = to_all(both[:, :1])
    d00_other = swap(d00, 1)
    d1x = to_all(both[:, 1:])
    d1x_other = swap(d1x, 1)

    piece = tiles[:16].reshape(2, 8, 4096).reshape(1, 2, 8, 4096)
    t = jnp.concatenate([piece, swap(piece, 8)])
    a1, a2, a3 = by_col(own)
    n1 = swap(t, 2, 16)
    n3 = swap(t, 6, 48)
    n2 = swap(n3, 2, 16)
    t = jnp.concatenate([t, n1, n2, n3])
    m1 = swap(t, 16, 2)
    m3 = swap(t, 48, 6)
    m2 = swap(m3, 16, 2)
    bufs = [t, m1, m2, m3]
    for v in list(bufs):
        bufs.append(swap(v, 1))
    slots = [
        [(16 * p + 2 * q + z + k, 16 * q + 2 * p + z + k, k) for q in range(4) for z in (0, 8)]
        for k in (0, 1)
        for p in range(4)
    ]

    square = jax.ShapeDtypeStruct((W, W), F32)
    wide = jax.ShapeDtypeStruct((256, 2 * W), F32)
    scratch = [pltpu.VMEM((W, 2 * W), F32), pltpu.VMEM((NB, NB), F32)]
    x0 = pl.pallas_call(
        first_kernel, out_shape=square, in_specs=[VM] * 2, out_specs=VM, scratch_shapes=scratch
    )(d00, d00_other)
    u01, x1 = pl.pallas_call(
        second_kernel,
        out_shape=[square, square],
        in_specs=[VM] * 3,
        out_specs=[VM] * 2,
        scratch_shapes=scratch,
    )(x0, d1x, d1x_other)
    b, g = pl.pallas_call(
        own_rows_kernel,
        out_shape=[wide, wide],
        in_specs=[VM] * 3 + [ANY] * 4,
        out_specs=[VM] * 2,
        scratch_shapes=[
            pltpu.VMEM((256, W), F32),
            pltpu.VMEM((256, W), F32),
            pltpu.SemaphoreType.DMA((2,)),
        ],
    )(x0, x1, u01, own, a1, a2, a3)
    result = pl.pallas_call(
        functools.partial(last_kernel, slots),
        out_shape=jax.ShapeDtypeStruct((256, 4, 8, 128), F32),
        in_specs=[ANY, VM, VM] + [ANY] * len(bufs),
        out_specs=ANY,
        scratch_shapes=[
            pltpu.VMEM((4, 1024, 1024), F32),
            pltpu.VMEM((4, 256, 8, 128), F32),
            pltpu.VMEM((3, 256, 1024), jnp.bfloat16),
            pltpu.SemaphoreType.DMA((4,)),
            pltpu.SemaphoreType.DMA((4,)),
            pltpu.SemaphoreType.DMA((4,)),
        ],
    )(tiles, b, g, *bufs)
    return result.transpose(0, 2, 1, 3).reshape(matrix.shape)


def solution(mesh):
    return jax.shard_map(
        steps,
        mesh=mesh,
        in_specs=(P(None, "row", None, "col"),),
        out_specs=P(None, "row", None, "col"),
        check_vma=False,
    )
```

profile of v0, /device:TPU:1, one launch (start us, length us, event | category | flops | bytes accessed | tf_op | source)
XLA Modules:
  0.0 241.9 jit_solution(13398428475888980029)
XLA Ops:
  1.0 7.8 %collective-permute-start.9 = (f32[1,2,8,4096]{3,2,1,0:T(8,128)S(1)}, f32[1,2,8,4096]{3,2,1,0:T(8,128)S(1)}, u32[]{:S(2)}, u32[]{:S(2)}) collective-permute-start(f32[1,2,8,4096]{3,2,1,0:T(8,128)S(1)} %reshape_reshape.3), channel_id=1, source_target_pairs={{0,32},{4,36},{8,40},{12,44},{16,48},{20,52},{24,56},{28,60},{32,0... | collective-permute-start | bytes 786440 | tf_op jit(solution)/shard_map/ppermute | solution.py:22
  8.9 6.5 %collective-permute-done.9 = f32[1,2,8,4096]{3,2,1,0:T(8,128)S(1)} collective-permute-done((f32[1,2,8,4096]{3,2,1,0:T(8,128)S(1)}, f32[1,2,8,4096]{3,2,1,0:T(8,128)S(1)}, u32[]{:S(2)}, u32[]{:S(2)}) %collective-permute-start.9) | collective-permute-done | bytes 262176 | tf_op jit(solution)/shard_map/ppermute | solution.py:22
  15.4 3.0 %collective-permute-start.11 = (f32[2,2,8,4096]{3,2,1,0:T(8,128)S(1)}, f32[2,2,8,4096]{3,2,1,0:T(8,128)S(1)}, u32[]{:S(2)}, u32[]{:S(2)}) collective-permute-start(f32[2,2,8,4096]{3,2,1,0:T(8,128)S(1)} %get-tuple-element.13), channel_id=1, source_target_pairs={{0,24},{4,196},{8,16},{12,204},{16,8},{20,212},{24,0},{28,220},{32... | collective-permute-start | bytes 1572872 | tf_op jit(solution)/shard_map/ppermute | solution.py:22
  18.5 6.9 %collective-permute-done.11 = f32[2,2,8,4096]{3,2,1,0:T(8,128)S(1)} collective-permute-done((f32[2,2,8,4096]{3,2,1,0:T(8,128)S(1)}, f32[2,2,8,4096]{3,2,1,0:T(8,128)S(1)}, u32[]{:S(2)}, u32[]{:S(2)}) %collective-permute-start.11) | collective-permute-done | bytes 524320 | tf_op jit(solution)/shard_map/ppermute | solution.py:22
  26.8 6.8 %collective-permute-done.12 = f32[2,2,8,4096]{3,2,1,0:T(8,128)S(1)} collective-permute-done((f32[2,2,8,4096]{3,2,1,0:T(8,128)S(1)}, f32[2,2,8,4096]{3,2,1,0:T(8,128)S(1)}, u32[]{:S(2)}, u32[]{:S(2)}) %collective-permute-start.12) | collective-permute-done | bytes 524320 | tf_op jit(solution)/shard_map/ppermute | solution.py:22
  33.7 3.0 %collective-permute-start.14 = (f32[8,2,8,4096]{3,2,1,0:T(8,128)S(1)}, f32[8,2,8,4096]{3,2,1,0:T(8,128)}, u32[]{:S(2)}, u32[]{:S(2)}) collective-permute-start(f32[8,2,8,4096]{3,2,1,0:T(8,128)S(1)} %constant_dynamic-update-slice_fusion.2.rest_0_), channel_id=1, source_target_pairs={{0,192},{4,28},{8,200},{12,20},{16,208},{20,12},{24,216},{28,4},{3... | collective-permute-start | bytes 6291464 | tf_op jit(solution)/shard_map/ppermute | solution.py:22
  36.8 23.8 %collective-permute-done.14.rest_3_ = f32[8,2,8,4096]{3,2,1,0:T(8,128)} collective-permute-done((f32[8,2,8,4096]{3,2,1,0:T(8,128)S(1)}, f32[8,2,8,4096]{3,2,1,0:T(8,128)}, u32[]{:S(2)}, u32[]{:S(2)}) %collective-permute-start.14) | collective-permute-done | bytes 2097184 | tf_op jit(solution)/shard_map/ppermute | solution.py:22
  61.6 5.5 %collective-permute-start.2 = (f32[16,512]{1,0:T(8,128)S(1)}, f32[16,512]{1,0:T(8,128)S(1)}, u32[]{:S(2)}, u32[]{:S(2)}) collective-permute-start(f32[16,512]{1,0:T(8,128)S(1)} %bitcast.29), channel_id=1, source_target_pairs={{0,3},{1,2},{4,7},{5,6},{8,11},{9,10},{12,15},{13,14},{16,19},{17,... | collective-permute-start | bytes 98312 | tf_op jit(solution)/shard_map/ppermute | solution.py:266
  67.0 3.9 %collective-permute-start.1 = (f32[16,512]{1,0:T(8,128)S(1)}, f32[16,512]{1,0:T(8,128)S(1)}, u32[]{:S(2)}, u32[]{:S(2)}) collective-permute-start(f32[16,512]{1,0:T(8,128)S(1)} %bitcast.30), channel_id=1, source_target_pairs={{0,2},{1,3},{4,6},{5,7},{8,10},{9,11},{12,14},{13,15},{16,18},{17,... | collective-permute-start | bytes 98312 | tf_op jit(solution)/shard_map/ppermute | solution.py:266
  71.0 2.2 collective-permute-start
  73.2 2.8 %collective-permute-done = f32[16,512]{1,0:T(8,128)S(1)} collective-permute-done((f32[16,512]{1,0:T(8,128)S(1)}, f32[16,512]{1,0:T(8,128)S(1)}, u32[]{:S(2)}, u32[]{:S(2)}) %collective-permute-start) | collective-permute-done | bytes 32800 | tf_op jit(solution)/shard_map/ppermute | solution.py:266
  76.1 4.9 %collective-permute-start.3 = (f32[3,8,512]{2,1,0:T(8,128)S(1)}, f32[3,8,512]{2,1,0:T(8,128)S(1)}, u32[]{:S(2)}, u32[]{:S(2)}) collective-permute-start(f32[3,8,512]{2,1,0:T(8,128)S(1)} %get-tuple-element.18), channel_id=1, source_target_pairs={{0,32},{4,36},{8,40},{12,44},{16,48},{20,52},{24,56},{28,60},{32,0... | collective-permute-start | bytes 147464 | tf_op jit(solution)/shard_map/ppermute | solution.py:22
  83.9 7.9 %all-to-all-start = ((f32[16,2,1,8,512]{4,3,2,1,0:T(8,128)}), f32[16,2,1,8,512]{4,3,2,1,0:T(8,128)S(1)}, u32[]{:S(2)}, u32[]{:S(2)}) async-start(f32[16,2,1,8,512]{4,3,2,1,0:T(8,128)} %broadcast_in_dim.6), calls=%async_computation | async-start | bytes 1048576 | tf_op jit(solution)/shard_map/all_to_all | solution.py:276
  91.8 2.7 %slice.38 = f32[32,8,1,512]{3,2,1,0:T(1,128)S(1)} slice(f32[32,8,8,512]{3,2,1,0:T(8,128)} %param.1), slice={[0:32], [0:8], [0:1], [0:512]} | slice | bytes 1048576 | tf_op jit(solution)/shard_map/slice | solution.py:262
  101.9 5.4 %all-to-all-start.1 = ((f32[16,2,2,8,512]{4,3,2,1,0:T(8,128)}), f32[16,2,2,8,512]{4,3,2,1,0:T(8,128)S(1)}, u32[]{:S(2)}, u32[]{:S(2)}) async-start(f32[16,2,2,8,512]{4,3,2,1,0:T(8,128)} %broadcast_in_dim.7), calls=%async_computation.1 | async-start | bytes 2097152 | tf_op jit(solution)/shard_map/all_to_all | solution.py:276
  107.3 7.7 %collective-permute-start.4 = (f32[16,2,1,8,512]{4,3,2,1,0:T(8,128)}, f32[16,2,1,8,512]{4,3,2,1,0:T(8,128)}, u32[]{:S(2)}, u32[]{:S(2)}) collective-permute-start(f32[16,2,1,8,512]{4,3,2,1,0:T(8,128)} %copy-done.2), channel_id=1, source_target_pairs={{0,4},{4,0},{8,12},{12,8},{16,20},{20,16},{24,28},{28,24},{32,36},... | collective-permute-start | bytes 1572872 | tf_op jit(solution)/shard_map/ppermute | solution.py:22
  115.2 5.1 %collective-permute-start.19 = (f32[8,2,8,4096]{3,2,1,0:T(8,128)}, f32[8,2,8,4096]{3,2,1,0:T(8,128)}, u32[]{:S(2)}, u32[]{:S(2)}) collective-permute-start(f32[8,2,8,4096]{3,2,1,0:T(8,128)} %collective-permute-done.14.rest_3_), channel_id=1, source_target_pairs={{0,4},{4,0},{8,12},{12,8},{16,20},{20,16},{24,28},{28,24},{32,36},... | collective-permute-start | bytes 6291464 | tf_op jit(solution)/shard_map/ppermute | solution.py:22
  120.9 7.0 %collective-permute-start.5 = (f32[16,2,2,8,512]{4,3,2,1,0:T(8,128)S(1)}, f32[16,2,2,8,512]{4,3,2,1,0:T(8,128)S(1)}, u32[]{:S(2)}, u32[]{:S(2)}) collective-permute-start(f32[16,2,2,8,512]{4,3,2,1,0:T(8,128)S(1)} %all-to-all-done.1.own), channel_id=1, source_target_pairs={{0,4},{4,0},{8,12},{12,8},{16,20},{20,16},{24,28},{28,24},{32,36},... | collective-permute-start | bytes 3145736 | tf_op jit(solution)/shard_map/ppermute | solution.py:22
  127.9 3.9 %collective-permute-done.5.other = f32[16,2,2,8,512]{4,3,2,1,0:T(8,128)S(1)} collective-permute-done((f32[16,2,2,8,512]{4,3,2,1,0:T(8,128)S(1)}, f32[16,2,2,8,512]{4,3,2,1,0:T(8,128)S(1)}, u32[]{:S(2)}, u32[]{:S(2)}) %collective-permute-start.5) | collective-permute-done | bytes 1048608 | tf_op jit(solution)/shard_map/ppermute | solution.py:22
  132.8 24.3 %collective-permute-start.6 = (f32[256,512]{1,0:T(8,128)}, f32[256,512]{1,0:T(8,128)}, u32[]{:S(2)}, u32[]{:S(2)}) collective-permute-start(f32[256,512]{1,0:T(8,128)} %bitcast.25.own), channel_id=1, source_target_pairs={{0,1},{1,0},{4,5},{5,4},{8,9},{9,8},{12,13},{13,12},{16,17},{17,16... | collective-permute-start | bytes 1572872 | tf_op jit(solution)/shard_map/ppermute | solution.py:266
  157.1 24.1 %shard_map.17.x0 = f32[512,512]{1,0:T(8,128)} custom-call(f32[16,2,1,8,512]{4,3,2,1,0:T(8,128)} %copy-done.2, f32[16,2,1,8,512]{4,3,2,1,0:T(8,128)} %collective-permute-done.4.other), custom_call_target="tpu_custom_call" | custom-call | tf_op jit(solution)/shard_map/pallas_call | solution.py:314
  181.2 29.0 %shard_map.18 = (f32[512,512]{1,0:T(8,128)}, f32[512,512]{1,0:T(8,128)}) custom-call(f32[512,512]{1,0:T(8,128)} %shard_map.17.x0, f32[16,2,2,8,512]{4,3,2,1,0:T(8,128)} %copy-done, f32[16,2,2,8,512]{4,3,2,1,0:T(8,128)} %copy-done.3), custom_call_target="tpu_custom_call" | custom-call | tf_op jit(solution)/shard_map/pallas_call | solution.py:317
  210.2 10.6 %shard_map.19 = (f32[256,1024]{1,0:T(8,128)}, f32[256,1024]{1,0:T(8,128)}) custom-call(f32[512,512]{1,0:T(8,128)} %shard_map.17.x0, f32[512,512]{1,0:T(8,128)} %get-tuple-element.9.x1, f32[512,512]{1,0:T(8,128)} %get-tuple-element.10.u01, f32[256,512]{1,0:T(8,128)} %bitcast.25.own, f32[256,512]{1,0:T(8,128)} %collective-permute-done.6.s1, ...), custom_call_target="tpu_custom_call" | custom-call | tf_op jit(solution)/shard_map/pallas_call | solution.py:324
  220.9 20.8 %shard_map.20 = f32[256,4,8,128]{3,2,1,0:T(8,128)} custom-call(f32[256,4,8,128]{3,2,1,0:T(8,128)} %bitcast.28, f32[256,1024]{1,0:T(8,128)} %get-tuple-element.11.b, f32[256,1024]{1,0:T(8,128)} %get-tuple-element.12.g, f32[8,2,8,4096]{3,2,1,0:T(8,128)} %copy-done.1, f32[8,2,8,4096]{3,2,1,0:T(8,128)} %collective-permute-done.13.rest_1_, ...), custom_call_target="tpu_custom_call" | custom-call | tf_op jit(solution)/shard_map/pallas_call | solution.py:335
  (51 shorter events, 15.6 us)
Async XLA Ops:
  1.0 14.4 %collective-permute-start.9 = (f32[1,2,8,4096]{3,2,1,0:T(8,128)S(1)}, f32[1,2,8,4096]{3,2,1,0:T(8,128)S(1)}, u32[]{:S(2)}, u32[]{:S(2)}) collective-permute-start(f32[1,2,8,4096]{3,2,1,0:T(8,128)S(1)} %reshape_reshape.3), channel_id=1, source_target_pairs={{0,32},{4,36},{8,40},{12,44},{16,48},{20,52},{24,56},{28,60},{32,0... | collective-permute-start | bytes 786440 | tf_op jit(solution)/shard_map/ppermute | solution.py:22
  15.4 9.9 %collective-permute-start.11 = (f32[2,2,8,4096]{3,2,1,0:T(8,128)S(1)}, f32[2,2,8,4096]{3,2,1,0:T(8,128)S(1)}, u32[]{:S(2)}, u32[]{:S(2)}) collective-permute-start(f32[2,2,8,4096]{3,2,1,0:T(8,128)S(1)} %get-tuple-element.13), channel_id=1, source_target_pairs={{0,24},{4,196},{8,16},{12,204},{16,8},{20,212},{24,0},{28,220},{32... | collective-permute-start | bytes 1572872 | tf_op jit(solution)/shard_map/ppermute | solution.py:22
  18.4 8.3 %collective-permute-start.10 = (f32[2,2,8,4096]{3,2,1,0:T(8,128)S(1)}, f32[2,2,8,4096]{3,2,1,0:T(8,128)S(1)}, u32[]{:S(2)}, u32[]{:S(2)}) collective-permute-start(f32[2,2,8,4096]{3,2,1,0:T(8,128)S(1)} %get-tuple-element.13), channel_id=1, source_target_pairs={{0,8},{4,68},{8,0},{12,76},{16,24},{20,84},{24,16},{28,92},{32,40}... | collective-permute-start | bytes 1572872 | tf_op jit(solution)/shard_map/ppermute | solution.py:22
  25.3 8.3 %collective-permute-start.12 = (f32[2,2,8,4096]{3,2,1,0:T(8,128)S(1)}, f32[2,2,8,4096]{3,2,1,0:T(8,128)S(1)}, u32[]{:S(2)}, u32[]{:S(2)}) collective-permute-start(f32[2,2,8,4096]{3,2,1,0:T(8,128)S(1)} %collective-permute-done.11), channel_id=1, source_target_pairs={{0,8},{4,68},{8,0},{12,76},{16,24},{20,84},{24,16},{28,92},{32,40}... | collective-permute-start | bytes 1572872 | tf_op jit(solution)/shard_map/ppermute | solution.py:22
  33.7 81.3 %copy-start.1 = (f32[8,2,8,4096]{3,2,1,0:T(8,128)}, f32[8,2,8,4096]{3,2,1,0:T(8,128)S(1)}, u32[]{:S(2)}) copy-start(f32[8,2,8,4096]{3,2,1,0:T(8,128)S(1)} %constant_dynamic-update-slice_fusion.2.rest_0_) | copy-start | bytes 6291460
  33.7 26.8 %collective-permute-start.14 = (f32[8,2,8,4096]{3,2,1,0:T(8,128)S(1)}, f32[8,2,8,4096]{3,2,1,0:T(8,128)}, u32[]{:S(2)}, u32[]{:S(2)}) collective-permute-start(f32[8,2,8,4096]{3,2,1,0:T(8,128)S(1)} %constant_dynamic-update-slice_fusion.2.rest_0_), channel_id=1, source_target_pairs={{0,192},{4,28},{8,200},{12,20},{16,208},{20,12},{24,216},{28,4},{3... | collective-permute-start | bytes 6291464 | tf_op jit(solution)/shard_map/ppermute | solution.py:22
  36.7 83.6 %collective-permute-start.13 = (f32[8,2,8,4096]{3,2,1,0:T(8,128)S(1)}, f32[8,2,8,4096]{3,2,1,0:T(8,128)}, u32[]{:S(2)}, u32[]{:S(2)}) collective-permute-start(f32[8,2,8,4096]{3,2,1,0:T(8,128)S(1)} %constant_dynamic-update-slice_fusion.2.rest_0_), channel_id=1, source_target_pairs={{0,64},{4,12},{8,72},{12,4},{16,80},{20,28},{24,88},{28,20},{32,96... | collective-permute-start | bytes 6291464 | tf_op jit(solution)/shard_map/ppermute | solution.py:22
  60.6 59.8 %collective-permute-start.15 = (f32[8,2,8,4096]{3,2,1,0:T(8,128)}, f32[8,2,8,4096]{3,2,1,0:T(8,128)}, u32[]{:S(2)}, u32[]{:S(2)}) collective-permute-start(f32[8,2,8,4096]{3,2,1,0:T(8,128)} %collective-permute-done.14.rest_3_), channel_id=1, source_target_pairs={{0,64},{4,12},{8,72},{12,4},{16,80},{20,28},{24,88},{28,20},{32,96... | collective-permute-start | bytes 6291464 | tf_op jit(solution)/shard_map/ppermute | solution.py:22
  61.6 11.6 %collective-permute-start.2 = (f32[16,512]{1,0:T(8,128)S(1)}, f32[16,512]{1,0:T(8,128)S(1)}, u32[]{:S(2)}, u32[]{:S(2)}) collective-permute-start(f32[16,512]{1,0:T(8,128)S(1)} %bitcast.29), channel_id=1, source_target_pairs={{0,3},{1,2},{4,7},{5,6},{8,11},{9,10},{12,15},{13,14},{16,19},{17,... | collective-permute-start | bytes 98312 | tf_op jit(solution)/shard_map/ppermute | solution.py:266
  67.0 6.2 %collective-permute-start.1 = (f32[16,512]{1,0:T(8,128)S(1)}, f32[16,512]{1,0:T(8,128)S(1)}, u32[]{:S(2)}, u32[]{:S(2)}) collective-permute-start(f32[16,512]{1,0:T(8,128)S(1)} %bitcast.30), channel_id=1, source_target_pairs={{0,2},{1,3},{4,6},{5,7},{8,10},{9,11},{12,14},{13,15},{16,18},{17,... | collective-permute-start | bytes 98312 | tf_op jit(solution)/shard_map/ppermute | solution.py:266
  71.0 5.1 %collective-permute-start = (f32[16,512]{1,0:T(8,128)S(1)}, f32[16,512]{1,0:T(8,128)S(1)}, u32[]{:S(2)}, u32[]{:S(2)}) collective-permute-start(f32[16,512]{1,0:T(8,128)S(1)} %bitcast.31), channel_id=1, source_target_pairs={{0,1},{1,0},{4,5},{5,4},{8,9},{9,8},{12,13},{13,12},{16,17},{17,16... | collective-permute-start | bytes 98312 | tf_op jit(solution)/shard_map/ppermute | solution.py:266
  76.1 6.9 %collective-permute-start.3 = (f32[3,8,512]{2,1,0:T(8,128)S(1)}, f32[3,8,512]{2,1,0:T(8,128)S(1)}, u32[]{:S(2)}, u32[]{:S(2)}) collective-permute-start(f32[3,8,512]{2,1,0:T(8,128)S(1)} %get-tuple-element.18), channel_id=1, source_target_pairs={{0,32},{4,36},{8,40},{12,44},{16,48},{20,52},{24,56},{28,60},{32,0... | collective-permute-start | bytes 147464 | tf_op jit(solution)/shard_map/ppermute | solution.py:22
  83.9 16.8 %all-to-all-start = ((f32[16,2,1,8,512]{4,3,2,1,0:T(8,128)}), f32[16,2,1,8,512]{4,3,2,1,0:T(8,128)S(1)}, u32[]{:S(2)}, u32[]{:S(2)}) async-start(f32[16,2,1,8,512]{4,3,2,1,0:T(8,128)} %broadcast_in_dim.6), calls=%async_computation | async-start | bytes 1048576 | tf_op jit(solution)/shard_map/all_to_all | solution.py:276
  95.3 19.7 %collective-permute-start.8 = (f32[256,512]{1,0:T(8,128)}, f32[256,512]{1,0:T(8,128)}, u32[]{:S(2)}, u32[]{:S(2)}) collective-permute-start(f32[256,512]{1,0:T(8,128)} %bitcast.25.own), channel_id=1, source_target_pairs={{0,3},{1,2},{4,7},{5,6},{8,11},{9,10},{12,15},{13,14},{16,19},{17,... | collective-permute-start | bytes 1572872 | tf_op jit(solution)/shard_map/ppermute | solution.py:266
  97.4 17.8 %collective-permute-start.7 = (f32[256,512]{1,0:T(8,128)}, f32[256,512]{1,0:T(8,128)}, u32[]{:S(2)}, u32[]{:S(2)}) collective-permute-start(f32[256,512]{1,0:T(8,128)} %bitcast.25.own), channel_id=1, source_target_pairs={{0,2},{1,3},{4,6},{5,7},{8,10},{9,11},{12,14},{13,15},{16,18},{17,... | collective-permute-start | bytes 1572872 | tf_op jit(solution)/shard_map/ppermute | solution.py:266
  101.9 19.0 %all-to-all-start.1 = ((f32[16,2,2,8,512]{4,3,2,1,0:T(8,128)}), f32[16,2,2,8,512]{4,3,2,1,0:T(8,128)S(1)}, u32[]{:S(2)}, u32[]{:S(2)}) async-start(f32[16,2,2,8,512]{4,3,2,1,0:T(8,128)} %broadcast_in_dim.7), calls=%async_computation.1 | async-start | bytes 2097152 | tf_op jit(solution)/shard_map/all_to_all | solution.py:276
  107.3 13.5 %collective-permute-start.4 = (f32[16,2,1,8,512]{4,3,2,1,0:T(8,128)}, f32[16,2,1,8,512]{4,3,2,1,0:T(8,128)}, u32[]{:S(2)}, u32[]{:S(2)}) collective-permute-start(f32[16,2,1,8,512]{4,3,2,1,0:T(8,128)} %copy-done.2), channel_id=1, source_target_pairs={{0,4},{4,0},{8,12},{12,8},{16,20},{20,16},{24,28},{28,24},{32,36},... | collective-permute-start | bytes 1572872 | tf_op jit(solution)/shard_map/ppermute | solution.py:22
  115.1 105.8 %collective-permute-start.16 = (f32[8,2,8,4096]{3,2,1,0:T(8,128)S(1)}, f32[8,2,8,4096]{3,2,1,0:T(8,128)}, u32[]{:S(2)}, u32[]{:S(2)}) collective-permute-start(f32[8,2,8,4096]{3,2,1,0:T(8,128)S(1)} %constant_dynamic-update-slice_fusion.2.rest_0_), channel_id=1, source_target_pairs={{0,4},{4,0},{8,12},{12,8},{16,20},{20,16},{24,28},{28,24},{32,36},... | collective-permute-start | bytes 6291464 | tf_op jit(solution)/shard_map/ppermute | solution.py:22
  115.2 105.7 %collective-permute-start.19 = (f32[8,2,8,4096]{3,2,1,0:T(8,128)}, f32[8,2,8,4096]{3,2,1,0:T(8,128)}, u32[]{:S(2)}, u32[]{:S(2)}) collective-permute-start(f32[8,2,8,4096]{3,2,1,0:T(8,128)} %collective-permute-done.14.rest_3_), channel_id=1, source_target_pairs={{0,4},{4,0},{8,12},{12,8},{16,20},{20,16},{24,28},{28,24},{32,36},... | collective-permute-start | bytes 6291464 | tf_op jit(solution)/shard_map/ppermute | solution.py:22
  120.3 100.6 %collective-permute-start.17 = (f32[8,2,8,4096]{3,2,1,0:T(8,128)}, f32[8,2,8,4096]{3,2,1,0:T(8,128)}, u32[]{:S(2)}, u32[]{:S(2)}) collective-permute-start(f32[8,2,8,4096]{3,2,1,0:T(8,128)} %collective-permute-done.13.rest_1_), channel_id=1, source_target_pairs={{0,4},{4,0},{8,12},{12,8},{16,20},{20,16},{24,28},{28,24},{32,36},... | collective-permute-start | bytes 6291464 | tf_op jit(solution)/shard_map/ppermute | solution.py:22
  120.3 100.6 %collective-permute-start.18 = (f32[8,2,8,4096]{3,2,1,0:T(8,128)}, f32[8,2,8,4096]{3,2,1,0:T(8,128)}, u32[]{:S(2)}, u32[]{:S(2)}) collective-permute-start(f32[8,2,8,4096]{3,2,1,0:T(8,128)} %collective-permute-done.15.rest_2_), channel_id=1, source_target_pairs={{0,4},{4,0},{8,12},{12,8},{16,20},{20,16},{24,28},{28,24},{32,36},... | collective-permute-start | bytes 6291464 | tf_op jit(solution)/shard_map/ppermute | solution.py:22
  120.8 60.4 %copy-start = (f32[16,2,2,8,512]{4,3,2,1,0:T(8,128)}, f32[16,2,2,8,512]{4,3,2,1,0:T(8,128)S(1)}, u32[]{:S(2)}) copy-start(f32[16,2,2,8,512]{4,3,2,1,0:T(8,128)S(1)} %all-to-all-done.1.own) | copy-start | bytes 3145732
  120.9 11.0 %collective-permute-start.5 = (f32[16,2,2,8,512]{4,3,2,1,0:T(8,128)S(1)}, f32[16,2,2,8,512]{4,3,2,1,0:T(8,128)S(1)}, u32[]{:S(2)}, u32[]{:S(2)}) collective-permute-start(f32[16,2,2,8,512]{4,3,2,1,0:T(8,128)S(1)} %all-to-all-done.1.own), channel_id=1, source_target_pairs={{0,4},{4,0},{8,12},{12,8},{16,20},{20,16},{24,28},{28,24},{32,36},... | collective-permute-start | bytes 3145736 | tf_op jit(solution)/shard_map/ppermute | solution.py:22
  132.8 77.5 %collective-permute-start.6 = (f32[256,512]{1,0:T(8,128)}, f32[256,512]{1,0:T(8,128)}, u32[]{:S(2)}, u32[]{:S(2)}) collective-permute-start(f32[256,512]{1,0:T(8,128)} %bitcast.25.own), channel_id=1, source_target_pairs={{0,1},{1,0},{4,5},{5,4},{8,9},{9,8},{12,13},{13,12},{16,17},{17,16... | collective-permute-start | bytes 1572872 | tf_op jit(solution)/shard_map/ppermute | solution.py:266
  (2 other events, 2.1 us)
where the time goes:
time: 243 us; the launch traced here: 242 us
  starting transfers between devices  92.9 us (38%)
  Pallas kernels  84.5 us (35%)
  waiting for transfers between devices  55.4 us (23%)
  local copies, waits for them, and re-layouts  8.67 us (4%)
    ppermute x14, waiting for transfers between devices, swap(): return lax.ppermute(value, 'row', pairs)  51.3 us
    ppermute x6, starting transfers between devices, send(): return lax.ppermute(value, 'col', list(pairs))  40.1 us
    ppermute x14, starting transfers between devices, swap(): return lax.ppermute(value, 'row', pairs)  39.4 us
    pallas_call x1, Pallas kernels, steps(): pl.pallas_call(second_kernel, out_shape=[square, square], in_specs=[VM] *...  29 us
    pallas_call x1, Pallas kernels, steps(): pl.pallas_call(first_kernel, out_shape=square, in_specs=[VM] * 2, out_spe...  24.1 us
    pallas_call x1, Pallas kernels, steps(): pl.pallas_call(functools.partial(last_kernel, slots), out_shape=jax.Shape...  20.8 us
    all_to_all x2, starting transfers between devices, to_all(): lax.all_to_all(copies, 'row', split_axis=0, concat_axis=0, axis_index_gro...  13.3 us
    pallas_call x1, Pallas kernels, steps(): pl.pallas_call(own_rows_kernel, out_shape=[wide, wide], in_specs=[VM] * 3...  10.6 us
  transfers between devices with their start and end apart: 22, of which 9 were waited for; matrix products, arithmetic and copies ran while one was open for 3% of the time, Pallas kernels for 26%

commit v1 on v0

--- a/solution.py
+++ b/solution.py
@@ -110,17 +110,14 @@
             inv[...], work[pl.ds(top, NB), pl.ds(nxt, W)]
         )
 
-        def update(i, carry):
-            at = pl.multiple_of(i * NB, NB)
-            work[pl.ds(at, NB), pl.ds(nxt, W)] -= dot(
-                work[pl.ds(top, NB), pl.ds(at, NB)],
-                work[pl.ds(top, NB), pl.ds(nxt, W)],
-                0,
-                0,
-            )
-            return carry
-
-        lax.fori_loop(kb + 1, W // NB, update, 0)
+        for k in range(W // NB - 1):
+
+            @pl.when(kb == k)
+            def _():
+                rows, now = slice((k + 1) * NB, W), slice(k * NB, (k + 1) * NB)
+                across = slice((k + 1) * NB, (k + 1) * NB + W)
+                work[rows, across] -= dot(work[now, rows], work[now, across], 0, 0)
+
         return carry
 
     lax.fori_loop(first, last, step, 0)
@@ -277,7 +274,7 @@
             copies, "row", split_axis=0, concat_axis=0, axis_index_groups=groups, tiled=True
         )
 
-    head = own[:16]
+    head = matrix[:2, :, 0, :].reshape(16, W)
     s1, s2, s3 = by_col(head)
     d0 = jnp.where(c == 0, head, jnp.where(c == 1, s1, jnp.where(c == 2, s2, s3)))
     d1 = jnp.where(c == 1, head, jnp.where(c == 0, s1, jnp.where(c == 3, s2, s3)))

time: 243 us -> 241 us (level)
  no operation moved by 1% of the time
where the time goes in v1:
time: 241 us
  starting transfers between devices  92.9 us (39%)
  Pallas kernels  83.2 us (35%)
  waiting for transfers between devices  55.4 us (23%)
  local copies, waits for them, and re-layouts  8.67 us (4%)
    ppermute x14, waiting for transfers between devices, swap(): return lax.ppermute(value, 'row', pairs)  51.3 us
    ppermute x6, starting transfers between devices, send(): return lax.ppermute(value, 'col', list(pairs))  40.1 us
    ppermute x14, starting transfers between devices, swap(): return lax.ppermute(value, 'row', pairs)  39.4 us
    pallas_call x1, Pallas kernels, steps(): pl.pallas_call(second_kernel, out_shape=[square, square], in_specs=[VM] *...  28.4 us
    pallas_call x1, Pallas kernels, steps(): pl.pallas_call(first_kernel, out_shape=square, in_specs=[VM] * 2, out_spe...  23.4 us
    pallas_call x1, Pallas kernels, steps(): pl.pallas_call(functools.partial(last_kernel, slots), out_shape=jax.Shape...  20.8 us
    all_to_all x2, starting transfers between devices, to_all(): lax.all_to_all(copies, 'row', split_axis=0, concat_axis=0, axis_index_gro...  13.3 us
    pallas_call x1, Pallas kernels, steps(): pl.pallas_call(own_rows_kernel, out_shape=[wide, wide], in_specs=[VM] * 3...  10.6 us
  transfers between devices with their start and end apart: 22, of which 9 were waited for; matrix products, arithmetic and copies ran while one was open for 3% of the time, Pallas kernels for 26%

profile of v1, /device:TPU:1, one launch (start us, length us, event | category | flops | bytes accessed | tf_op | source)
XLA Modules:
  0.0 240.6 jit_solution(14524576626725107789)
XLA Ops:
  1.0 7.8 %collective-permute-start.9 = (f32[1,2,8,4096]{3,2,1,0:T(8,128)S(1)}, f32[1,2,8,4096]{3,2,1,0:T(8,128)S(1)}, u32[]{:S(2)}, u32[]{:S(2)}) collective-permute-start(f32[1,2,8,4096]{3,2,1,0:T(8,128)S(1)} %reshape_reshape.3), channel_id=1, source_target_pairs={{0,32},{4,36},{8,40},{12,44},{16,48},{20,52},{24,56},{28,60},{32,0... | collective-permute-start | bytes 786440 | tf_op jit(solution)/shard_map/ppermute | solution.py:22
  8.9 6.5 %collective-permute-done.9 = f32[1,2,8,4096]{3,2,1,0:T(8,128)S(1)} collective-permute-done((f32[1,2,8,4096]{3,2,1,0:T(8,128)S(1)}, f32[1,2,8,4096]{3,2,1,0:T(8,128)S(1)}, u32[]{:S(2)}, u32[]{:S(2)}) %collective-permute-start.9) | collective-permute-done | bytes 262176 | tf_op jit(solution)/shard_map/ppermute | solution.py:22
  15.4 3.0 %collective-permute-start.11 = (f32[2,2,8,4096]{3,2,1,0:T(8,128)S(1)}, f32[2,2,8,4096]{3,2,1,0:T(8,128)S(1)}, u32[]{:S(2)}, u32[]{:S(2)}) collective-permute-start(f32[2,2,8,4096]{3,2,1,0:T(8,128)S(1)} %get-tuple-element.13), channel_id=1, source_target_pairs={{0,24},{4,196},{8,16},{12,204},{16,8},{20,212},{24,0},{28,220},{32... | collective-permute-start | bytes 1572872 | tf_op jit(solution)/shard_map/ppermute | solution.py:22
  18.5 6.9 %collective-permute-done.11 = f32[2,2,8,4096]{3,2,1,0:T(8,128)S(1)} collective-permute-done((f32[2,2,8,4096]{3,2,1,0:T(8,128)S(1)}, f32[2,2,8,4096]{3,2,1,0:T(8,128)S(1)}, u32[]{:S(2)}, u32[]{:S(2)}) %collective-permute-start.11) | collective-permute-done | bytes 524320 | tf_op jit(solution)/shard_map/ppermute | solution.py:22
  26.8 6.8 %collective-permute-done.12 = f32[2,2,8,4096]{3,2,1,0:T(8,128)S(1)} collective-permute-done((f32[2,2,8,4096]{3,2,1,0:T(8,128)S(1)}, f32[2,2,8,4096]{3,2,1,0:T(8,128)S(1)}, u32[]{:S(2)}, u32[]{:S(2)}) %collective-permute-start.12) | collective-permute-done | bytes 524320 | tf_op jit(solution)/shard_map/ppermute | solution.py:22
  33.7 3.0 %collective-permute-start.14 = (f32[8,2,8,4096]{3,2,1,0:T(8,128)S(1)}, f32[8,2,8,4096]{3,2,1,0:T(8,128)}, u32[]{:S(2)}, u32[]{:S(2)}) collective-permute-start(f32[8,2,8,4096]{3,2,1,0:T(8,128)S(1)} %constant_dynamic-update-slice_fusion.2.rest_0_), channel_id=1, source_target_pairs={{0,192},{4,28},{8,200},{12,20},{16,208},{20,12},{24,216},{28,4},{3... | collective-permute-start | bytes 6291464 | tf_op jit(solution)/shard_map/ppermute | solution.py:22
  36.8 23.8 %collective-permute-done.14.rest_3_ = f32[8,2,8,4096]{3,2,1,0:T(8,128)} collective-permute-done((f32[8,2,8,4096]{3,2,1,0:T(8,128)S(1)}, f32[8,2,8,4096]{3,2,1,0:T(8,128)}, u32[]{:S(2)}, u32[]{:S(2)}) %collective-permute-start.14) | collective-permute-done | bytes 2097184 | tf_op jit(solution)/shard_map/ppermute | solution.py:22
  61.6 5.5 %collective-permute-start.2 = (f32[16,512]{1,0:T(8,128)S(1)}, f32[16,512]{1,0:T(8,128)S(1)}, u32[]{:S(2)}, u32[]{:S(2)}) collective-permute-start(f32[16,512]{1,0:T(8,128)S(1)} %bitcast.29), channel_id=1, source_target_pairs={{0,3},{1,2},{4,7},{5,6},{8,11},{9,10},{12,15},{13,14},{16,19},{17,... | collective-permute-start | bytes 98312 | tf_op jit(solution)/shard_map/ppermute | solution.py:263
  67.0 3.9 %collective-permute-start.1 = (f32[16,512]{1,0:T(8,128)S(1)}, f32[16,512]{1,0:T(8,128)S(1)}, u32[]{:S(2)}, u32[]{:S(2)}) collective-permute-start(f32[16,512]{1,0:T(8,128)S(1)} %bitcast.30), channel_id=1, source_target_pairs={{0,2},{1,3},{4,6},{5,7},{8,10},{9,11},{12,14},{13,15},{16,18},{17,... | collective-permute-start | bytes 98312 | tf_op jit(solution)/shard_map/ppermute | solution.py:263
  71.0 2.2 collective-permute-start
  73.2 2.8 %collective-permute-done = f32[16,512]{1,0:T(8,128)S(1)} collective-permute-done((f32[16,512]{1,0:T(8,128)S(1)}, f32[16,512]{1,0:T(8,128)S(1)}, u32[]{:S(2)}, u32[]{:S(2)}) %collective-permute-start) | collective-permute-done | bytes 32800 | tf_op jit(solution)/shard_map/ppermute | solution.py:263
  76.1 4.9 %collective-permute-start.3 = (f32[3,8,512]{2,1,0:T(8,128)S(1)}, f32[3,8,512]{2,1,0:T(8,128)S(1)}, u32[]{:S(2)}, u32[]{:S(2)}) collective-permute-start(f32[3,8,512]{2,1,0:T(8,128)S(1)} %get-tuple-element.18), channel_id=1, source_target_pairs={{0,32},{4,36},{8,40},{12,44},{16,48},{20,52},{24,56},{28,60},{32,0... | collective-permute-start | bytes 147464 | tf_op jit(solution)/shard_map/ppermute | solution.py:22
  83.9 7.9 %all-to-all-start = ((f32[16,2,1,8,512]{4,3,2,1,0:T(8,128)}), f32[16,2,1,8,512]{4,3,2,1,0:T(8,128)S(1)}, u32[]{:S(2)}, u32[]{:S(2)}) async-start(f32[16,2,1,8,512]{4,3,2,1,0:T(8,128)} %broadcast_in_dim.6), calls=%async_computation | async-start | bytes 1048576 | tf_op jit(solution)/shard_map/all_to_all | solution.py:273
  91.8 2.7 %slice.33 = f32[32,8,1,512]{3,2,1,0:T(1,128)S(1)} slice(f32[32,8,8,512]{3,2,1,0:T(8,128)} %param.1), slice={[0:32], [0:8], [0:1], [0:512]} | slice | bytes 1048576 | tf_op jit(solution)/shard_map/slice | solution.py:259
  101.9 5.4 %all-to-all-start.1 = ((f32[16,2,2,8,512]{4,3,2,1,0:T(8,128)}), f32[16,2,2,8,512]{4,3,2,1,0:T(8,128)S(1)}, u32[]{:S(2)}, u32[]{:S(2)}) async-start(f32[16,2,2,8,512]{4,3,2,1,0:T(8,128)} %broadcast_in_dim.7), calls=%async_computation.1 | async-start | bytes 2097152 | tf_op jit(solution)/shard_map/all_to_all | solution.py:273
  107.3 7.7 %collective-permute-start.4 = (f32[16,2,1,8,512]{4,3,2,1,0:T(8,128)}, f32[16,2,1,8,512]{4,3,2,1,0:T(8,128)}, u32[]{:S(2)}, u32[]{:S(2)}) collective-permute-start(f32[16,2,1,8,512]{4,3,2,1,0:T(8,128)} %copy-done.2), channel_id=1, source_target_pairs={{0,4},{4,0},{8,12},{12,8},{16,20},{20,16},{24,28},{28,24},{32,36},... | collective-permute-start | bytes 1572872 | tf_op jit(solution)/shard_map/ppermute | solution.py:22
  115.2 5.1 %collective-permute-start.19 = (f32[8,2,8,4096]{3,2,1,0:T(8,128)}, f32[8,2,8,4096]{3,2,1,0:T(8,128)}, u32[]{:S(2)}, u32[]{:S(2)}) collective-permute-start(f32[8,2,8,4096]{3,2,1,0:T(8,128)} %collective-permute-done.14.rest_3_), channel_id=1, source_target_pairs={{0,4},{4,0},{8,12},{12,8},{16,20},{20,16},{24,28},{28,24},{32,36},... | collective-permute-start | bytes 6291464 | tf_op jit(solution)/shard_map/ppermute | solution.py:22
  120.9 7.0 %collective-permute-start.5 = (f32[16,2,2,8,512]{4,3,2,1,0:T(8,128)S(1)}, f32[16,2,2,8,512]{4,3,2,1,0:T(8,128)S(1)}, u32[]{:S(2)}, u32[]{:S(2)}) collective-permute-start(f32[16,2,2,8,512]{4,3,2,1,0:T(8,128)S(1)} %all-to-all-done.1.own), channel_id=1, source_target_pairs={{0,4},{4,0},{8,12},{12,8},{16,20},{20,16},{24,28},{28,24},{32,36},... | collective-permute-start | bytes 3145736 | tf_op jit(solution)/shard_map/ppermute | solution.py:22
  127.9 3.9 %collective-permute-done.5.other = f32[16,2,2,8,512]{4,3,2,1,0:T(8,128)S(1)} collective-permute-done((f32[16,2,2,8,512]{4,3,2,1,0:T(8,128)S(1)}, f32[16,2,2,8,512]{4,3,2,1,0:T(8,128)S(1)}, u32[]{:S(2)}, u32[]{:S(2)}) %collective-permute-start.5) | collective-permute-done | bytes 1048608 | tf_op jit(solution)/shard_map/ppermute | solution.py:22
  132.8 24.3 %collective-permute-start.6 = (f32[256,512]{1,0:T(8,128)}, f32[256,512]{1,0:T(8,128)}, u32[]{:S(2)}, u32[]{:S(2)}) collective-permute-start(f32[256,512]{1,0:T(8,128)} %bitcast.25.own), channel_id=1, source_target_pairs={{0,1},{1,0},{4,5},{5,4},{8,9},{9,8},{12,13},{13,12},{16,17},{17,16... | collective-permute-start | bytes 1572872 | tf_op jit(solution)/shard_map/ppermute | solution.py:263
  157.1 23.4 %shard_map.17.x0 = f32[512,512]{1,0:T(8,128)} custom-call(f32[16,2,1,8,512]{4,3,2,1,0:T(8,128)} %copy-done.2, f32[16,2,1,8,512]{4,3,2,1,0:T(8,128)} %collective-permute-done.4.other), custom_call_target="tpu_custom_call" | custom-call | tf_op jit(solution)/shard_map/pallas_call | solution.py:311
  180.6 28.4 %shard_map.18 = (f32[512,512]{1,0:T(8,128)}, f32[512,512]{1,0:T(8,128)}) custom-call(f32[512,512]{1,0:T(8,128)} %shard_map.17.x0, f32[16,2,2,8,512]{4,3,2,1,0:T(8,128)} %copy-done, f32[16,2,2,8,512]{4,3,2,1,0:T(8,128)} %copy-done.3), custom_call_target="tpu_custom_call" | custom-call | tf_op jit(solution)/shard_map/pallas_call | solution.py:314
  209.0 10.6 %shard_map.19 = (f32[256,1024]{1,0:T(8,128)}, f32[256,1024]{1,0:T(8,128)}) custom-call(f32[512,512]{1,0:T(8,128)} %shard_map.17.x0, f32[512,512]{1,0:T(8,128)} %get-tuple-element.9.x1, f32[512,512]{1,0:T(8,128)} %get-tuple-element.10.u01, f32[256,512]{1,0:T(8,128)} %bitcast.25.own, f32[256,512]{1,0:T(8,128)} %collective-permute-done.6.s1, ...), custom_call_target="tpu_custom_call" | custom-call | tf_op jit(solution)/shard_map/pallas_call | solution.py:321
  219.6 20.8 %shard_map.20 = f32[256,4,8,128]{3,2,1,0:T(8,128)} custom-call(f32[256,4,8,128]{3,2,1,0:T(8,128)} %bitcast.28, f32[256,1024]{1,0:T(8,128)} %get-tuple-element.11.b, f32[256,1024]{1,0:T(8,128)} %get-tuple-element.12.g, f32[8,2,8,4096]{3,2,1,0:T(8,128)} %copy-done.1, f32[8,2,8,4096]{3,2,1,0:T(8,128)} %collective-permute-done.13.rest_1_, ...), custom_call_target="tpu_custom_call" | custom-call | tf_op jit(solution)/shard_map/pallas_call | solution.py:332
  (51 shorter events, 15.6 us)
Async XLA Ops:
  1.0 14.4 %collective-permute-start.9 = (f32[1,2,8,4096]{3,2,1,0:T(8,128)S(1)}, f32[1,2,8,4096]{3,2,1,0:T(8,128)S(1)}, u32[]{:S(2)}, u32[]{:S(2)}) collective-permute-start(f32[1,2,8,4096]{3,2,1,0:T(8,128)S(1)} %reshape_reshape.3), channel_id=1, source_target_pairs={{0,32},{4,36},{8,40},{12,44},{16,48},{20,52},{24,56},{28,60},{32,0... | collective-permute-start | bytes 786440 | tf_op jit(solution)/shard_map/ppermute | solution.py:22
  15.4 9.9 %collective-permute-start.11 = (f32[2,2,8,4096]{3,2,1,0:T(8,128)S(1)}, f32[2,2,8,4096]{3,2,1,0:T(8,128)S(1)}, u32[]{:S(2)}, u32[]{:S(2)}) collective-permute-start(f32[2,2,8,4096]{3,2,1,0:T(8,128)S(1)} %get-tuple-element.13), channel_id=1, source_target_pairs={{0,24},{4,196},{8,16},{12,204},{16,8},{20,212},{24,0},{28,220},{32... | collective-permute-start | bytes 1572872 | tf_op jit(solution)/shard_map/ppermute | solution.py:22
  18.4 8.3 %collective-permute-start.10 = (f32[2,2,8,4096]{3,2,1,0:T(8,128)S(1)}, f32[2,2,8,4096]{3,2,1,0:T(8,128)S(1)}, u32[]{:S(2)}, u32[]{:S(2)}) collective-permute-start(f32[2,2,8,4096]{3,2,1,0:T(8,128)S(1)} %get-tuple-element.13), channel_id=1, source_target_pairs={{0,8},{4,68},{8,0},{12,76},{16,24},{20,84},{24,16},{28,92},{32,40}... | collective-permute-start | bytes 1572872 | tf_op jit(solution)/shard_map/ppermute | solution.py:22
  25.3 8.3 %collective-permute-start.12 = (f32[2,2,8,4096]{3,2,1,0:T(8,128)S(1)}, f32[2,2,8,4096]{3,2,1,0:T(8,128)S(1)}, u32[]{:S(2)}, u32[]{:S(2)}) collective-permute-start(f32[2,2,8,4096]{3,2,1,0:T(8,128)S(1)} %collective-permute-done.11), channel_id=1, source_target_pairs={{0,8},{4,68},{8,0},{12,76},{16,24},{20,84},{24,16},{28,92},{32,40}... | collective-permute-start | bytes 1572872 | tf_op jit(solution)/shard_map/ppermute | solution.py:22
  33.7 81.3 %copy-start.1 = (f32[8,2,8,4096]{3,2,1,0:T(8,128)}, f32[8,2,8,4096]{3,2,1,0:T(8,128)S(1)}, u32[]{:S(2)}) copy-start(f32[8,2,8,4096]{3,2,1,0:T(8,128)S(1)} %constant_dynamic-update-slice_fusion.2.rest_0_) | copy-start | bytes 6291460
  33.7 26.8 %collective-permute-start.14 = (f32[8,2,8,4096]{3,2,1,0:T(8,128)S(1)}, f32[8,2,8,4096]{3,2,1,0:T(8,128)}, u32[]{:S(2)}, u32[]{:S(2)}) collective-permute-start(f32[8,2,8,4096]{3,2,1,0:T(8,128)S(1)} %constant_dynamic-update-slice_fusion.2.rest_0_), channel_id=1, source_target_pairs={{0,192},{4,28},{8,200},{12,20},{16,208},{20,12},{24,216},{28,4},{3... | collective-permute-start | bytes 6291464 | tf_op jit(solution)/shard_map/ppermute | solution.py:22
  36.7 83.6 %collective-permute-start.13 = (f32[8,2,8,4096]{3,2,1,0:T(8,128)S(1)}, f32[8,2,8,4096]{3,2,1,0:T(8,128)}, u32[]{:S(2)}, u32[]{:S(2)}) collective-permute-start(f32[8,2,8,4096]{3,2,1,0:T(8,128)S(1)} %constant_dynamic-update-slice_fusion.2.rest_0_), channel_id=1, source_target_pairs={{0,64},{4,12},{8,72},{12,4},{16,80},{20,28},{24,88},{28,20},{32,96... | collective-permute-start | bytes 6291464 | tf_op jit(solution)/shard_map/ppermute | solution.py:22
  60.6 59.8 %collective-permute-start.15 = (f32[8,2,8,4096]{3,2,1,0:T(8,128)}, f32[8,2,8,4096]{3,2,1,0:T(8,128)}, u32[]{:S(2)}, u32[]{:S(2)}) collective-permute-start(f32[8,2,8,4096]{3,2,1,0:T(8,128)} %collective-permute-done.14.rest_3_), channel_id=1, source_target_pairs={{0,64},{4,12},{8,72},{12,4},{16,80},{20,28},{24,88},{28,20},{32,96... | collective-permute-start | bytes 6291464 | tf_op jit(solution)/shard_map/ppermute | solution.py:22
  61.6 11.6 %collective-permute-start.2 = (f32[16,512]{1,0:T(8,128)S(1)}, f32[16,512]{1,0:T(8,128)S(1)}, u32[]{:S(2)}, u32[]{:S(2)}) collective-permute-start(f32[16,512]{1,0:T(8,128)S(1)} %bitcast.29), channel_id=1, source_target_pairs={{0,3},{1,2},{4,7},{5,6},{8,11},{9,10},{12,15},{13,14},{16,19},{17,... | collective-permute-start | bytes 98312 | tf_op jit(solution)/shard_map/ppermute | solution.py:263
  67.0 6.2 %collective-permute-start.1 = (f32[16,512]{1,0:T(8,128)S(1)}, f32[16,512]{1,0:T(8,128)S(1)}, u32[]{:S(2)}, u32[]{:S(2)}) collective-permute-start(f32[16,512]{1,0:T(8,128)S(1)} %bitcast.30), channel_id=1, source_target_pairs={{0,2},{1,3},{4,6},{5,7},{8,10},{9,11},{12,14},{13,15},{16,18},{17,... | collective-permute-start | bytes 98312 | tf_op jit(solution)/shard_map/ppermute | solution.py:263
  71.0 5.1 %collective-permute-start = (f32[16,512]{1,0:T(8,128)S(1)}, f32[16,512]{1,0:T(8,128)S(1)}, u32[]{:S(2)}, u32[]{:S(2)}) collective-permute-start(f32[16,512]{1,0:T(8,128)S(1)} %bitcast.31), channel_id=1, source_target_pairs={{0,1},{1,0},{4,5},{5,4},{8,9},{9,8},{12,13},{13,12},{16,17},{17,16... | collective-permute-start | bytes 98312 | tf_op jit(solution)/shard_map/ppermute | solution.py:263
  76.1 6.9 %collective-permute-start.3 = (f32[3,8,512]{2,1,0:T(8,128)S(1)}, f32[3,8,512]{2,1,0:T(8,128)S(1)}, u32[]{:S(2)}, u32[]{:S(2)}) collective-permute-start(f32[3,8,512]{2,1,0:T(8,128)S(1)} %get-tuple-element.18), channel_id=1, source_target_pairs={{0,32},{4,36},{8,40},{12,44},{16,48},{20,52},{24,56},{28,60},{32,0... | collective-permute-start | bytes 147464 | tf_op jit(solution)/shard_map/ppermute | solution.py:22
  83.9 16.8 %all-to-all-start = ((f32[16,2,1,8,512]{4,3,2,1,0:T(8,128)}), f32[16,2,1,8,512]{4,3,2,1,0:T(8,128)S(1)}, u32[]{:S(2)}, u32[]{:S(2)}) async-start(f32[16,2,1,8,512]{4,3,2,1,0:T(8,128)} %broadcast_in_dim.6), calls=%async_computation | async-start | bytes 1048576 | tf_op jit(solution)/shard_map/all_to_all | solution.py:273
  95.3 19.7 %collective-permute-start.8 = (f32[256,512]{1,0:T(8,128)}, f32[256,512]{1,0:T(8,128)}, u32[]{:S(2)}, u32[]{:S(2)}) collective-permute-start(f32[256,512]{1,0:T(8,128)} %bitcast.25.own), channel_id=1, source_target_pairs={{0,3},{1,2},{4,7},{5,6},{8,11},{9,10},{12,15},{13,14},{16,19},{17,... | collective-permute-start | bytes 1572872 | tf_op jit(solution)/shard_map/ppermute | solution.py:263
  97.4 17.8 %collective-permute-start.7 = (f32[256,512]{1,0:T(8,128)}, f32[256,512]{1,0:T(8,128)}, u32[]{:S(2)}, u32[]{:S(2)}) collective-permute-start(f32[256,512]{1,0:T(8,128)} %bitcast.25.own), channel_id=1, source_target_pairs={{0,2},{1,3},{4,6},{5,7},{8,10},{9,11},{12,14},{13,15},{16,18},{17,... | collective-permute-start | bytes 1572872 | tf_op jit(solution)/shard_map/ppermute | solution.py:263
  101.9 19.0 %all-to-all-start.1 = ((f32[16,2,2,8,512]{4,3,2,1,0:T(8,128)}), f32[16,2,2,8,512]{4,3,2,1,0:T(8,128)S(1)}, u32[]{:S(2)}, u32[]{:S(2)}) async-start(f32[16,2,2,8,512]{4,3,2,1,0:T(8,128)} %broadcast_in_dim.7), calls=%async_computation.1 | async-start | bytes 2097152 | tf_op jit(solution)/shard_map/all_to_all | solution.py:273
  107.3 13.5 %collective-permute-start.4 = (f32[16,2,1,8,512]{4,3,2,1,0:T(8,128)}, f32[16,2,1,8,512]{4,3,2,1,0:T(8,128)}, u32[]{:S(2)}, u32[]{:S(2)}) collective-permute-start(f32[16,2,1,8,512]{4,3,2,1,0:T(8,128)} %copy-done.2), channel_id=1, source_target_pairs={{0,4},{4,0},{8,12},{12,8},{16,20},{20,16},{24,28},{28,24},{32,36},... | collective-permute-start | bytes 1572872 | tf_op jit(solution)/shard_map/ppermute | solution.py:22
  115.1 104.5 %collective-permute-start.16 = (f32[8,2,8,4096]{3,2,1,0:T(8,128)S(1)}, f32[8,2,8,4096]{3,2,1,0:T(8,128)}, u32[]{:S(2)}, u32[]{:S(2)}) collective-permute-start(f32[8,2,8,4096]{3,2,1,0:T(8,128)S(1)} %constant_dynamic-update-slice_fusion.2.rest_0_), channel_id=1, source_target_pairs={{0,4},{4,0},{8,12},{12,8},{16,20},{20,16},{24,28},{28,24},{32,36},... | collective-permute-start | bytes 6291464 | tf_op jit(solution)/shard_map/ppermute | solution.py:22
  115.2 104.4 %collective-permute-start.19 = (f32[8,2,8,4096]{3,2,1,0:T(8,128)}, f32[8,2,8,4096]{3,2,1,0:T(8,128)}, u32[]{:S(2)}, u32[]{:S(2)}) collective-permute-start(f32[8,2,8,4096]{3,2,1,0:T(8,128)} %collective-permute-done.14.rest_3_), channel_id=1, source_target_pairs={{0,4},{4,0},{8,12},{12,8},{16,20},{20,16},{24,28},{28,24},{32,36},... | collective-permute-start | bytes 6291464 | tf_op jit(solution)/shard_map/ppermute | solution.py:22
  120.3 99.3 %collective-permute-start.17 = (f32[8,2,8,4096]{3,2,1,0:T(8,128)}, f32[8,2,8,4096]{3,2,1,0:T(8,128)}, u32[]{:S(2)}, u32[]{:S(2)}) collective-permute-start(f32[8,2,8,4096]{3,2,1,0:T(8,128)} %collective-permute-done.13.rest_1_), channel_id=1, source_target_pairs={{0,4},{4,0},{8,12},{12,8},{16,20},{20,16},{24,28},{28,24},{32,36},... | collective-permute-start | bytes 6291464 | tf_op jit(solution)/shard_map/ppermute | solution.py:22
  120.3 99.3 %collective-permute-start.18 = (f32[8,2,8,4096]{3,2,1,0:T(8,128)}, f32[8,2,8,4096]{3,2,1,0:T(8,128)}, u32[]{:S(2)}, u32[]{:S(2)}) collective-permute-start(f32[8,2,8,4096]{3,2,1,0:T(8,128)} %collective-permute-done.15.rest_2_), channel_id=1, source_target_pairs={{0,4},{4,0},{8,12},{12,8},{16,20},{20,16},{24,28},{28,24},{32,36},... | collective-permute-start | bytes 6291464 | tf_op jit(solution)/shard_map/ppermute | solution.py:22
  120.8 59.7 %copy-start = (f32[16,2,2,8,512]{4,3,2,1,0:T(8,128)}, f32[16,2,2,8,512]{4,3,2,1,0:T(8,128)S(1)}, u32[]{:S(2)}) copy-start(f32[16,2,2,8,512]{4,3,2,1,0:T(8,128)S(1)} %all-to-all-done.1.own) | copy-start | bytes 3145732
  120.9 11.0 %collective-permute-start.5 = (f32[16,2,2,8,512]{4,3,2,1,0:T(8,128)S(1)}, f32[16,2,2,8,512]{4,3,2,1,0:T(8,128)S(1)}, u32[]{:S(2)}, u32[]{:S(2)}) collective-permute-start(f32[16,2,2,8,512]{4,3,2,1,0:T(8,128)S(1)} %all-to-all-done.1.own), channel_id=1, source_target_pairs={{0,4},{4,0},{8,12},{12,8},{16,20},{20,16},{24,28},{28,24},{32,36},... | collective-permute-start | bytes 3145736 | tf_op jit(solution)/shard_map/ppermute | solution.py:22
  132.8 76.2 %collective-permute-start.6 = (f32[256,512]{1,0:T(8,128)}, f32[256,512]{1,0:T(8,128)}, u32[]{:S(2)}, u32[]{:S(2)}) collective-permute-start(f32[256,512]{1,0:T(8,128)} %bitcast.25.own), channel_id=1, source_target_pairs={{0,1},{1,0},{4,5},{5,4},{8,9},{9,8},{12,13},{13,12},{16,17},{17,16... | collective-permute-start | bytes 1572872 | tf_op jit(solution)/shard_map/ppermute | solution.py:263
  (2 other events, 2.1 us)

commit v2 on v1

--- a/solution.py
+++ b/solution.py
@@ -9,6 +9,7 @@
 
 
 W = 512
+H = W // 2
 NB = 128
 F32 = jnp.float32
 HI = lax.Precision.HIGHEST
@@ -143,11 +144,21 @@
 def second_kernel(x0, own, other, u01, x1, work, inv):
     lay_out(work, slice(W, 2 * W), own, other, 0)
     lay_out(work, slice(0, W), own, other, 1)
-    u01[...] = dot(x0[...], work[:, W:], 1, 1)
-    work[:, :W] -= dot(u01[...], u01[...], 0, 0)
+    u01[:H, :] = dot(x0[:H, :H], work[:, W : W + H], 1, 1)
+    u01[H:, :] = dot(x0[H:, :], work[:, W:], 1, 1)
+    work[:H, :W] -= dot(u01[:, :H], u01[...], 0, 0)
+    work[H:, H:W] -= dot(u01[:, H:], u01[:, H:], 0, 0)
     identity(work)
     factor_steps(work, inv, 0, 4)
     x1[...] = work[:, W:]
+
+
+def times_inverse_t(a, x):
+    return jnp.concatenate([dot(a[:, :H], x[:H, :H], 1, 1), dot(a, x[H:, :], 1, 1)], axis=1)
+
+
+def times_inverse(a, x):
+    return jnp.concatenate([dot(a, x[:, :H]), dot(a[:, H:], x[H:, H:])], axis=1)
 
 
 def own_rows_kernel(x0, x1, u01, own, s1, s2, s3, b, g, a0, a1, sem):
@@ -159,14 +170,15 @@
             def _():
                 pltpu.make_async_copy(source, dst, sem.at[k]).start()
 
-        pltpu.make_async_copy(own, dst, sem.at[k]).wait()
-    b0 = dot(a0[...], x0[...], 1, 1)
-    b1 = dot(a1[...] - dot(b0, u01[...]), x1[...], 1, 1)
-    g1 = dot(b1, x1[...])
+    pltpu.make_async_copy(own, a0, sem.at[0]).wait()
+    b0 = times_inverse_t(a0[...], x0)
+    pltpu.make_async_copy(own, a1, sem.at[1]).wait()
+    b1 = times_inverse_t(a1[...] - dot(b0, u01[...]), x1)
+    g1 = times_inverse(b1, x1)
     b[:, :W] = b0
     b[:, W:] = b1
     g[:, W:] = g1
-    g[:, :W] = dot(b0 - dot(g1, u01[...], 1, 1), x0[...])
+    g[:, :W] = times_inverse(b0 - dot(g1, u01[...], 1, 1), x0)
 
 
 def thirds(v):
@@ -231,7 +243,7 @@
                 flat[at, :] = jnp.where((row < 16) & trailing, F32(0), value)
             return carry
 
-        lax.fori_loop(0, 2, some, 0)
+        lax.fori_loop(0, 2, some, 0, unroll=2)
 
         @pl.when(c < 2)
         def _():

time: 241 us -> 239 us (level)
  transfers between devices with their start and end apart: 22 -> 22, of which waited for: 9 -> 9; matrix products, arithmetic and copies ran while one was open for 3% -> 3% of each run, Pallas kernels for 26% -> 25%
where the time goes in v2:
time: 239 us; the launch traced here: 238 us
  starting transfers between devices  92.9 us (39%)
  Pallas kernels  80.9 us (34%)
  waiting for transfers between devices  55.4 us (23%)
  local copies, waits for them, and re-layouts  8.67 us (4%)
    ppermute x14, waiting for transfers between devices, swap(): return lax.ppermute(value, 'row', pairs)  51.3 us
    ppermute x6, starting transfers between devices, send(): return lax.ppermute(value, 'col', list(pairs))  40.1 us
    ppermute x14, starting transfers between devices, swap(): return lax.ppermute(value, 'row', pairs)  39.4 us
    pallas_call x1, Pallas kernels, steps(): pl.pallas_call(second_kernel, out_shape=[square, square], in_specs=[VM] *...  27.6 us
    pallas_call x1, Pallas kernels, steps(): pl.pallas_call(first_kernel, out_shape=square, in_specs=[VM] * 2, out_spe...  23.4 us
    pallas_call x1, Pallas kernels, steps(): pl.pallas_call(functools.partial(last_kernel, slots), out_shape=jax.Shape...  20.3 us
    all_to_all x2, starting transfers between devices, to_all(): lax.all_to_all(copies, 'row', split_axis=0, concat_axis=0, axis_index_gro...  13.3 us
    pallas_call x1, Pallas kernels, steps(): pl.pallas_call(own_rows_kernel, out_shape=[wide, wide], in_specs=[VM] * 3...  9.61 us
  transfers between devices with their start and end apart: 22, of which 9 were waited for; matrix products, arithmetic and copies ran while one was open for 3% of the time, Pallas kernels for 25%

profile of v2, /device:TPU:1, one launch (start us, length us, event | category | flops | bytes accessed | tf_op | source)
XLA Modules:
  0.0 238.3 jit_solution(1202361888842544989)
XLA Ops:
  1.0 7.8 %collective-permute-start.9 = (f32[1,2,8,4096]{3,2,1,0:T(8,128)S(1)}, f32[1,2,8,4096]{3,2,1,0:T(8,128)S(1)}, u32[]{:S(2)}, u32[]{:S(2)}) collective-permute-start(f32[1,2,8,4096]{3,2,1,0:T(8,128)S(1)} %reshape_reshape.3), channel_id=1, source_target_pairs={{0,32},{4,36},{8,40},{12,44},{16,48},{20,52},{24,56},{28,60},{32,0... | collective-permute-start | bytes 786440 | tf_op jit(solution)/shard_map/ppermute | solution.py:23
  8.9 6.5 %collective-permute-done.9 = f32[1,2,8,4096]{3,2,1,0:T(8,128)S(1)} collective-permute-done((f32[1,2,8,4096]{3,2,1,0:T(8,128)S(1)}, f32[1,2,8,4096]{3,2,1,0:T(8,128)S(1)}, u32[]{:S(2)}, u32[]{:S(2)}) %collective-permute-start.9) | collective-permute-done | bytes 262176 | tf_op jit(solution)/shard_map/ppermute | solution.py:23
  15.4 3.0 %collective-permute-start.11 = (f32[2,2,8,4096]{3,2,1,0:T(8,128)S(1)}, f32[2,2,8,4096]{3,2,1,0:T(8,128)S(1)}, u32[]{:S(2)}, u32[]{:S(2)}) collective-permute-start(f32[2,2,8,4096]{3,2,1,0:T(8,128)S(1)} %get-tuple-element.13), channel_id=1, source_target_pairs={{0,24},{4,196},{8,16},{12,204},{16,8},{20,212},{24,0},{28,220},{32... | collective-permute-start | bytes 1572872 | tf_op jit(solution)/shard_map/ppermute | solution.py:23
  18.5 6.9 %collective-permute-done.11 = f32[2,2,8,4096]{3,2,1,0:T(8,128)S(1)} collective-permute-done((f32[2,2,8,4096]{3,2,1,0:T(8,128)S(1)}, f32[2,2,8,4096]{3,2,1,0:T(8,128)S(1)}, u32[]{:S(2)}, u32[]{:S(2)}) %collective-permute-start.11) | collective-permute-done | bytes 524320 | tf_op jit(solution)/shard_map/ppermute | solution.py:23
  26.8 6.8 %collective-permute-done.12 = f32[2,2,8,4096]{3,2,1,0:T(8,128)S(1)} collective-permute-done((f32[2,2,8,4096]{3,2,1,0:T(8,128)S(1)}, f32[2,2,8,4096]{3,2,1,0:T(8,128)S(1)}, u32[]{:S(2)}, u32[]{:S(2)}) %collective-permute-start.12) | collective-permute-done | bytes 524320 | tf_op jit(solution)/shard_map/ppermute | solution.py:23
  33.7 3.0 %collective-permute-start.14 = (f32[8,2,8,4096]{3,2,1,0:T(8,128)S(1)}, f32[8,2,8,4096]{3,2,1,0:T(8,128)}, u32[]{:S(2)}, u32[]{:S(2)}) collective-permute-start(f32[8,2,8,4096]{3,2,1,0:T(8,128)S(1)} %constant_dynamic-update-slice_fusion.2.rest_0_), channel_id=1, source_target_pairs={{0,192},{4,28},{8,200},{12,20},{16,208},{20,12},{24,216},{28,4},{3... | collective-permute-start | bytes 6291464 | tf_op jit(solution)/shard_map/ppermute | solution.py:23
  36.8 23.8 %collective-permute-done.14.rest_3_ = f32[8,2,8,4096]{3,2,1,0:T(8,128)} collective-permute-done((f32[8,2,8,4096]{3,2,1,0:T(8,128)S(1)}, f32[8,2,8,4096]{3,2,1,0:T(8,128)}, u32[]{:S(2)}, u32[]{:S(2)}) %collective-permute-start.14) | collective-permute-done | bytes 2097184 | tf_op jit(solution)/shard_map/ppermute | solution.py:23
  61.6 5.5 %collective-permute-start.2 = (f32[16,512]{1,0:T(8,128)S(1)}, f32[16,512]{1,0:T(8,128)S(1)}, u32[]{:S(2)}, u32[]{:S(2)}) collective-permute-start(f32[16,512]{1,0:T(8,128)S(1)} %bitcast.29), channel_id=1, source_target_pairs={{0,3},{1,2},{4,7},{5,6},{8,11},{9,10},{12,15},{13,14},{16,19},{17,... | collective-permute-start | bytes 98312 | tf_op jit(solution)/shard_map/ppermute | solution.py:275
  67.0 3.9 %collective-permute-start.1 = (f32[16,512]{1,0:T(8,128)S(1)}, f32[16,512]{1,0:T(8,128)S(1)}, u32[]{:S(2)}, u32[]{:S(2)}) collective-permute-start(f32[16,512]{1,0:T(8,128)S(1)} %bitcast.30), channel_id=1, source_target_pairs={{0,2},{1,3},{4,6},{5,7},{8,10},{9,11},{12,14},{13,15},{16,18},{17,... | collective-permute-start | bytes 98312 | tf_op jit(solution)/shard_map/ppermute | solution.py:275
  71.0 2.2 collective-permute-start
  73.2 2.8 %collective-permute-done = f32[16,512]{1,0:T(8,128)S(1)} collective-permute-done((f32[16,512]{1,0:T(8,128)S(1)}, f32[16,512]{1,0:T(8,128)S(1)}, u32[]{:S(2)}, u32[]{:S(2)}) %collective-permute-start) | collective-permute-done | bytes 32800 | tf_op jit(solution)/shard_map/ppermute | solution.py:275
  76.1 4.9 %collective-permute-start.3 = (f32[3,8,512]{2,1,0:T(8,128)S(1)}, f32[3,8,512]{2,1,0:T(8,128)S(1)}, u32[]{:S(2)}, u32[]{:S(2)}) collective-permute-start(f32[3,8,512]{2,1,0:T(8,128)S(1)} %get-tuple-element.18), channel_id=1, source_target_pairs={{0,32},{4,36},{8,40},{12,44},{16,48},{20,52},{24,56},{28,60},{32,0... | collective-permute-start | bytes 147464 | tf_op jit(solution)/shard_map/ppermute | solution.py:23
  83.9 7.9 %all-to-all-start = ((f32[16,2,1,8,512]{4,3,2,1,0:T(8,128)}), f32[16,2,1,8,512]{4,3,2,1,0:T(8,128)S(1)}, u32[]{:S(2)}, u32[]{:S(2)}) async-start(f32[16,2,1,8,512]{4,3,2,1,0:T(8,128)} %broadcast_in_dim.6), calls=%async_computation | async-start | bytes 1048576 | tf_op jit(solution)/shard_map/all_to_all | solution.py:285
  91.8 2.7 %slice.33 = f32[32,8,1,512]{3,2,1,0:T(1,128)S(1)} slice(f32[32,8,8,512]{3,2,1,0:T(8,128)} %param.1), slice={[0:32], [0:8], [0:1], [0:512]} | slice | bytes 1048576 | tf_op jit(solution)/shard_map/slice | solution.py:271
  101.9 5.4 %all-to-all-start.1 = ((f32[16,2,2,8,512]{4,3,2,1,0:T(8,128)}), f32[16,2,2,8,512]{4,3,2,1,0:T(8,128)S(1)}, u32[]{:S(2)}, u32[]{:S(2)}) async-start(f32[16,2,2,8,512]{4,3,2,1,0:T(8,128)} %broadcast_in_dim.7), calls=%async_computation.1 | async-start | bytes 2097152 | tf_op jit(solution)/shard_map/all_to_all | solution.py:285
  107.3 7.7 %collective-permute-start.4 = (f32[16,2,1,8,512]{4,3,2,1,0:T(8,128)}, f32[16,2,1,8,512]{4,3,2,1,0:T(8,128)}, u32[]{:S(2)}, u32[]{:S(2)}) collective-permute-start(f32[16,2,1,8,512]{4,3,2,1,0:T(8,128)} %copy-done.2), channel_id=1, source_target_pairs={{0,4},{4,0},{8,12},{12,8},{16,20},{20,16},{24,28},{28,24},{32,36},... | collective-permute-start | bytes 1572872 | tf_op jit(solution)/shard_map/ppermute | solution.py:23
  115.2 5.1 %collective-permute-start.19 = (f32[8,2,8,4096]{3,2,1,0:T(8,128)}, f32[8,2,8,4096]{3,2,1,0:T(8,128)}, u32[]{:S(2)}, u32[]{:S(2)}) collective-permute-start(f32[8,2,8,4096]{3,2,1,0:T(8,128)} %collective-permute-done.14.rest_3_), channel_id=1, source_target_pairs={{0,4},{4,0},{8,12},{12,8},{16,20},{20,16},{24,28},{28,24},{32,36},... | collective-permute-start | bytes 6291464 | tf_op jit(solution)/shard_map/ppermute | solution.py:23
  120.9 7.0 %collective-permute-start.5 = (f32[16,2,2,8,512]{4,3,2,1,0:T(8,128)S(1)}, f32[16,2,2,8,512]{4,3,2,1,0:T(8,128)S(1)}, u32[]{:S(2)}, u32[]{:S(2)}) collective-permute-start(f32[16,2,2,8,512]{4,3,2,1,0:T(8,128)S(1)} %all-to-all-done.1.own), channel_id=1, source_target_pairs={{0,4},{4,0},{8,12},{12,8},{16,20},{20,16},{24,28},{28,24},{32,36},... | collective-permute-start | bytes 3145736 | tf_op jit(solution)/shard_map/ppermute | solution.py:23
  127.9 3.9 %collective-permute-done.5.other = f32[16,2,2,8,512]{4,3,2,1,0:T(8,128)S(1)} collective-permute-done((f32[16,2,2,8,512]{4,3,2,1,0:T(8,128)S(1)}, f32[16,2,2,8,512]{4,3,2,1,0:T(8,128)S(1)}, u32[]{:S(2)}, u32[]{:S(2)}) %collective-permute-start.5) | collective-permute-done | bytes 1048608 | tf_op jit(solution)/shard_map/ppermute | solution.py:23
  132.8 24.3 %collective-permute-start.6 = (f32[256,512]{1,0:T(8,128)}, f32[256,512]{1,0:T(8,128)}, u32[]{:S(2)}, u32[]{:S(2)}) collective-permute-start(f32[256,512]{1,0:T(8,128)} %bitcast.25.own), channel_id=1, source_target_pairs={{0,1},{1,0},{4,5},{5,4},{8,9},{9,8},{12,13},{13,12},{16,17},{17,16... | collective-permute-start | bytes 1572872 | tf_op jit(solution)/shard_map/ppermute | solution.py:275
  157.1 23.4 %shard_map.17.x0 = f32[512,512]{1,0:T(8,128)} custom-call(f32[16,2,1,8,512]{4,3,2,1,0:T(8,128)} %copy-done.2, f32[16,2,1,8,512]{4,3,2,1,0:T(8,128)} %collective-permute-done.4.other), custom_call_target="tpu_custom_call" | custom-call | tf_op jit(solution)/shard_map/pallas_call | solution.py:323
  180.6 27.6 %shard_map.18 = (f32[512,512]{1,0:T(8,128)}, f32[512,512]{1,0:T(8,128)}) custom-call(f32[512,512]{1,0:T(8,128)} %shard_map.17.x0, f32[16,2,2,8,512]{4,3,2,1,0:T(8,128)} %copy-done, f32[16,2,2,8,512]{4,3,2,1,0:T(8,128)} %copy-done.3), custom_call_target="tpu_custom_call" | custom-call | tf_op jit(solution)/shard_map/pallas_call | solution.py:326
  208.2 9.6 %shard_map.19 = (f32[256,1024]{1,0:T(8,128)}, f32[256,1024]{1,0:T(8,128)}) custom-call(f32[512,512]{1,0:T(8,128)} %shard_map.17.x0, f32[512,512]{1,0:T(8,128)} %get-tuple-element.9.x1, f32[512,512]{1,0:T(8,128)} %get-tuple-element.10.u01, f32[256,512]{1,0:T(8,128)} %bitcast.25.own, f32[256,512]{1,0:T(8,128)} %collective-permute-done.6.s1, ...), custom_call_target="tpu_custom_call" | custom-call | tf_op jit(solution)/shard_map/pallas_call | solution.py:333
  217.8 20.3 %shard_map.20 = f32[256,4,8,128]{3,2,1,0:T(8,128)} custom-call(f32[256,4,8,128]{3,2,1,0:T(8,128)} %bitcast.28, f32[256,1024]{1,0:T(8,128)} %get-tuple-element.11.b, f32[256,1024]{1,0:T(8,128)} %get-tuple-element.12.g, f32[8,2,8,4096]{3,2,1,0:T(8,128)} %copy-done.1, f32[8,2,8,4096]{3,2,1,0:T(8,128)} %collective-permute-done.13.rest_1_, ...), custom_call_target="tpu_custom_call" | custom-call | tf_op jit(solution)/shard_map/pallas_call | solution.py:344
  (51 shorter events, 15.6 us)
Async XLA Ops:
  1.0 14.4 %collective-permute-start.9 = (f32[1,2,8,4096]{3,2,1,0:T(8,128)S(1)}, f32[1,2,8,4096]{3,2,1,0:T(8,128)S(1)}, u32[]{:S(2)}, u32[]{:S(2)}) collective-permute-start(f32[1,2,8,4096]{3,2,1,0:T(8,128)S(1)} %reshape_reshape.3), channel_id=1, source_target_pairs={{0,32},{4,36},{8,40},{12,44},{16,48},{20,52},{24,56},{28,60},{32,0... | collective-permute-start | bytes 786440 | tf_op jit(solution)/shard_map/ppermute | solution.py:23
  15.4 9.9 %collective-permute-start.11 = (f32[2,2,8,4096]{3,2,1,0:T(8,128)S(1)}, f32[2,2,8,4096]{3,2,1,0:T(8,128)S(1)}, u32[]{:S(2)}, u32[]{:S(2)}) collective-permute-start(f32[2,2,8,4096]{3,2,1,0:T(8,128)S(1)} %get-tuple-element.13), channel_id=1, source_target_pairs={{0,24},{4,196},{8,16},{12,204},{16,8},{20,212},{24,0},{28,220},{32... | collective-permute-start | bytes 1572872 | tf_op jit(solution)/shard_map/ppermute | solution.py:23
  18.4 8.3 %collective-permute-start.10 = (f32[2,2,8,4096]{3,2,1,0:T(8,128)S(1)}, f32[2,2,8,4096]{3,2,1,0:T(8,128)S(1)}, u32[]{:S(2)}, u32[]{:S(2)}) collective-permute-start(f32[2,2,8,4096]{3,2,1,0:T(8,128)S(1)} %get-tuple-element.13), channel_id=1, source_target_pairs={{0,8},{4,68},{8,0},{12,76},{16,24},{20,84},{24,16},{28,92},{32,40}... | collective-permute-start | bytes 1572872 | tf_op jit(solution)/shard_map/ppermute | solution.py:23
  25.3 8.3 %collective-permute-start.12 = (f32[2,2,8,4096]{3,2,1,0:T(8,128)S(1)}, f32[2,2,8,4096]{3,2,1,0:T(8,128)S(1)}, u32[]{:S(2)}, u32[]{:S(2)}) collective-permute-start(f32[2,2,8,4096]{3,2,1,0:T(8,128)S(1)} %collective-permute-done.11), channel_id=1, source_target_pairs={{0,8},{4,68},{8,0},{12,76},{16,24},{20,84},{24,16},{28,92},{32,40}... | collective-permute-start | bytes 1572872 | tf_op jit(solution)/shard_map/ppermute | solution.py:23
  33.7 81.3 %copy-start.1 = (f32[8,2,8,4096]{3,2,1,0:T(8,128)}, f32[8,2,8,4096]{3,2,1,0:T(8,128)S(1)}, u32[]{:S(2)}) copy-start(f32[8,2,8,4096]{3,2,1,0:T(8,128)S(1)} %constant_dynamic-update-slice_fusion.2.rest_0_) | copy-start | bytes 6291460
  33.7 26.8 %collective-permute-start.14 = (f32[8,2,8,4096]{3,2,1,0:T(8,128)S(1)}, f32[8,2,8,4096]{3,2,1,0:T(8,128)}, u32[]{:S(2)}, u32[]{:S(2)}) collective-permute-start(f32[8,2,8,4096]{3,2,1,0:T(8,128)S(1)} %constant_dynamic-update-slice_fusion.2.rest_0_), channel_id=1, source_target_pairs={{0,192},{4,28},{8,200},{12,20},{16,208},{20,12},{24,216},{28,4},{3... | collective-permute-start | bytes 6291464 | tf_op jit(solution)/shard_map/ppermute | solution.py:23
  36.7 83.6 %collective-permute-start.13 = (f32[8,2,8,4096]{3,2,1,0:T(8,128)S(1)}, f32[8,2,8,4096]{3,2,1,0:T(8,128)}, u32[]{:S(2)}, u32[]{:S(2)}) collective-permute-start(f32[8,2,8,4096]{3,2,1,0:T(8,128)S(1)} %constant_dynamic-update-slice_fusion.2.rest_0_), channel_id=1, source_target_pairs={{0,64},{4,12},{8,72},{12,4},{16,80},{20,28},{24,88},{28,20},{32,96... | collective-permute-start | bytes 6291464 | tf_op jit(solution)/shard_map/ppermute | solution.py:23
  60.6 59.8 %collective-permute-start.15 = (f32[8,2,8,4096]{3,2,1,0:T(8,128)}, f32[8,2,8,4096]{3,2,1,0:T(8,128)}, u32[]{:S(2)}, u32[]{:S(2)}) collective-permute-start(f32[8,2,8,4096]{3,2,1,0:T(8,128)} %collective-permute-done.14.rest_3_), channel_id=1, source_target_pairs={{0,64},{4,12},{8,72},{12,4},{16,80},{20,28},{24,88},{28,20},{32,96... | collective-permute-start | bytes 6291464 | tf_op jit(solution)/shard_map/ppermute | solution.py:23
  61.6 11.6 %collective-permute-start.2 = (f32[16,512]{1,0:T(8,128)S(1)}, f32[16,512]{1,0:T(8,128)S(1)}, u32[]{:S(2)}, u32[]{:S(2)}) collective-permute-start(f32[16,512]{1,0:T(8,128)S(1)} %bitcast.29), channel_id=1, source_target_pairs={{0,3},{1,2},{4,7},{5,6},{8,11},{9,10},{12,15},{13,14},{16,19},{17,... | collective-permute-start | bytes 98312 | tf_op jit(solution)/shard_map/ppermute | solution.py:275
  67.0 6.2 %collective-permute-start.1 = (f32[16,512]{1,0:T(8,128)S(1)}, f32[16,512]{1,0:T(8,128)S(1)}, u32[]{:S(2)}, u32[]{:S(2)}) collective-permute-start(f32[16,512]{1,0:T(8,128)S(1)} %bitcast.30), channel_id=1, source_target_pairs={{0,2},{1,3},{4,6},{5,7},{8,10},{9,11},{12,14},{13,15},{16,18},{17,... | collective-permute-start | bytes 98312 | tf_op jit(solution)/shard_map/ppermute | solution.py:275
  71.0 5.1 %collective-permute-start = (f32[16,512]{1,0:T(8,128)S(1)}, f32[16,512]{1,0:T(8,128)S(1)}, u32[]{:S(2)}, u32[]{:S(2)}) collective-permute-start(f32[16,512]{1,0:T(8,128)S(1)} %bitcast.31), channel_id=1, source_target_pairs={{0,1},{1,0},{4,5},{5,4},{8,9},{9,8},{12,13},{13,12},{16,17},{17,16... | collective-permute-start | bytes 98312 | tf_op jit(solution)/shard_map/ppermute | solution.py:275
  76.1 6.9 %collective-permute-start.3 = (f32[3,8,512]{2,1,0:T(8,128)S(1)}, f32[3,8,512]{2,1,0:T(8,128)S(1)}, u32[]{:S(2)}, u32[]{:S(2)}) collective-permute-start(f32[3,8,512]{2,1,0:T(8,128)S(1)} %get-tuple-element.18), channel_id=1, source_target_pairs={{0,32},{4,36},{8,40},{12,44},{16,48},{20,52},{24,56},{28,60},{32,0... | collective-permute-start | bytes 147464 | tf_op jit(solution)/shard_map/ppermute | solution.py:23
  83.9 16.8 %all-to-all-start = ((f32[16,2,1,8,512]{4,3,2,1,0:T(8,128)}), f32[16,2,1,8,512]{4,3,2,1,0:T(8,128)S(1)}, u32[]{:S(2)}, u32[]{:S(2)}) async-start(f32[16,2,1,8,512]{4,3,2,1,0:T(8,128)} %broadcast_in_dim.6), calls=%async_computation | async-start | bytes 1048576 | tf_op jit(solution)/shard_map/all_to_all | solution.py:285
  95.3 19.7 %collective-permute-start.8 = (f32[256,512]{1,0:T(8,128)}, f32[256,512]{1,0:T(8,128)}, u32[]{:S(2)}, u32[]{:S(2)}) collective-permute-start(f32[256,512]{1,0:T(8,128)} %bitcast.25.own), channel_id=1, source_target_pairs={{0,3},{1,2},{4,7},{5,6},{8,11},{9,10},{12,15},{13,14},{16,19},{17,... | collective-permute-start | bytes 1572872 | tf_op jit(solution)/shard_map/ppermute | solution.py:275
  97.4 17.8 %collective-permute-start.7 = (f32[256,512]{1,0:T(8,128)}, f32[256,512]{1,0:T(8,128)}, u32[]{:S(2)}, u32[]{:S(2)}) collective-permute-start(f32[256,512]{1,0:T(8,128)} %bitcast.25.own), channel_id=1, source_target_pairs={{0,2},{1,3},{4,6},{5,7},{8,10},{9,11},{12,14},{13,15},{16,18},{17,... | collective-permute-start | bytes 1572872 | tf_op jit(solution)/shard_map/ppermute | solution.py:275
  101.9 19.0 %all-to-all-start.1 = ((f32[16,2,2,8,512]{4,3,2,1,0:T(8,128)}), f32[16,2,2,8,512]{4,3,2,1,0:T(8,128)S(1)}, u32[]{:S(2)}, u32[]{:S(2)}) async-start(f32[16,2,2,8,512]{4,3,2,1,0:T(8,128)} %broadcast_in_dim.7), calls=%async_computation.1 | async-start | bytes 2097152 | tf_op jit(solution)/shard_map/all_to_all | solution.py:285
  107.3 13.5 %collective-permute-start.4 = (f32[16,2,1,8,512]{4,3,2,1,0:T(8,128)}, f32[16,2,1,8,512]{4,3,2,1,0:T(8,128)}, u32[]{:S(2)}, u32[]{:S(2)}) collective-permute-start(f32[16,2,1,8,512]{4,3,2,1,0:T(8,128)} %copy-done.2), channel_id=1, source_target_pairs={{0,4},{4,0},{8,12},{12,8},{16,20},{20,16},{24,28},{28,24},{32,36},... | collective-permute-start | bytes 1572872 | tf_op jit(solution)/shard_map/ppermute | solution.py:23
  115.1 102.7 %collective-permute-start.16 = (f32[8,2,8,4096]{3,2,1,0:T(8,128)S(1)}, f32[8,2,8,4096]{3,2,1,0:T(8,128)}, u32[]{:S(2)}, u32[]{:S(2)}) collective-permute-start(f32[8,2,8,4096]{3,2,1,0:T(8,128)S(1)} %constant_dynamic-update-slice_fusion.2.rest_0_), channel_id=1, source_target_pairs={{0,4},{4,0},{8,12},{12,8},{16,20},{20,16},{24,28},{28,24},{32,36},... | collective-permute-start | bytes 6291464 | tf_op jit(solution)/shard_map/ppermute | solution.py:23
  115.2 102.6 %collective-permute-start.19 = (f32[8,2,8,4096]{3,2,1,0:T(8,128)}, f32[8,2,8,4096]{3,2,1,0:T(8,128)}, u32[]{:S(2)}, u32[]{:S(2)}) collective-permute-start(f32[8,2,8,4096]{3,2,1,0:T(8,128)} %collective-permute-done.14.rest_3_), channel_id=1, source_target_pairs={{0,4},{4,0},{8,12},{12,8},{16,20},{20,16},{24,28},{28,24},{32,36},... | collective-permute-start | bytes 6291464 | tf_op jit(solution)/shard_map/ppermute | solution.py:23
  120.3 97.5 %collective-permute-start.17 = (f32[8,2,8,4096]{3,2,1,0:T(8,128)}, f32[8,2,8,4096]{3,2,1,0:T(8,128)}, u32[]{:S(2)}, u32[]{:S(2)}) collective-permute-start(f32[8,2,8,4096]{3,2,1,0:T(8,128)} %collective-permute-done.13.rest_1_), channel_id=1, source_target_pairs={{0,4},{4,0},{8,12},{12,8},{16,20},{20,16},{24,28},{28,24},{32,36},... | collective-permute-start | bytes 6291464 | tf_op jit(solution)/shard_map/ppermute | solution.py:23
  120.3 97.5 %collective-permute-start.18 = (f32[8,2,8,4096]{3,2,1,0:T(8,128)}, f32[8,2,8,4096]{3,2,1,0:T(8,128)}, u32[]{:S(2)}, u32[]{:S(2)}) collective-permute-start(f32[8,2,8,4096]{3,2,1,0:T(8,128)} %collective-permute-done.15.rest_2_), channel_id=1, source_target_pairs={{0,4},{4,0},{8,12},{12,8},{16,20},{20,16},{24,28},{28,24},{32,36},... | collective-permute-start | bytes 6291464 | tf_op jit(solution)/shard_map/ppermute | solution.py:23
  120.8 59.7 %copy-start = (f32[16,2,2,8,512]{4,3,2,1,0:T(8,128)}, f32[16,2,2,8,512]{4,3,2,1,0:T(8,128)S(1)}, u32[]{:S(2)}) copy-start(f32[16,2,2,8,512]{4,3,2,1,0:T(8,128)S(1)} %all-to-all-done.1.own) | copy-start | bytes 3145732
  120.9 11.0 %collective-permute-start.5 = (f32[16,2,2,8,512]{4,3,2,1,0:T(8,128)S(1)}, f32[16,2,2,8,512]{4,3,2,1,0:T(8,128)S(1)}, u32[]{:S(2)}, u32[]{:S(2)}) collective-permute-start(f32[16,2,2,8,512]{4,3,2,1,0:T(8,128)S(1)} %all-to-all-done.1.own), channel_id=1, source_target_pairs={{0,4},{4,0},{8,12},{12,8},{16,20},{20,16},{24,28},{28,24},{32,36},... | collective-permute-start | bytes 3145736 | tf_op jit(solution)/shard_map/ppermute | solution.py:23
  132.8 75.4 %collective-permute-start.6 = (f32[256,512]{1,0:T(8,128)}, f32[256,512]{1,0:T(8,128)}, u32[]{:S(2)}, u32[]{:S(2)}) collective-permute-start(f32[256,512]{1,0:T(8,128)} %bitcast.25.own), channel_id=1, source_target_pairs={{0,1},{1,0},{4,5},{5,4},{8,9},{9,8},{12,13},{13,12},{16,17},{17,16... | collective-permute-start | bytes 1572872 | tf_op jit(solution)/shard_map/ppermute | solution.py:275
  (2 other events, 2.1 us)
